TPU v7x, 32 devices: a whole 2x2x4 slice. The times are simulated.
32 devices in a mesh: gx: 4 (over z), gy: 8 (over y, x, core).
Axes of the slice: x: 2, y: 2, z: 4, core: 2. Of those that a mesh axis runs over, the one named last changes fastest.
Arguments:
- vorticity: float32 [8192, 8192], P('gx', 'gy'), may hold values from -6 to 6
- tile_list: int32 [32, 16], P(('gx', 'gy')), may hold values from 0 to 4095, as said below
- float_slot: int32 [65536], P(('gx', 'gy')), may hold values from 0 to 15, as said below
- float_cell: int32 [2, 65536], P(None, ('gx', 'gy')), may hold values from 1 to 125
- float_frac: float32 [2, 65536], P(None, ('gx', 'gy')), may hold values from 0 to 1
Outputs:
- float_velocity: float32 [2, 65536], P(None, ('gx', 'gy'))
Inputs may be any that keep to these rules, and one draw needn't show every extreme that they name: `tile_list`: row b lists the 16 tiles used by float block b; tile t covers the 128 x 128 cells from row (t // 64) * 128 and column (t % 64) * 128. The 16 tiles of a row lie in the blocks of vorticity held by 16 different devices, and one device's block is named by every row. `float_slot`: at most 256 floats of one block name the same position; in every block the position whose tile lies in the device block named by every row of tile_list is named by exactly 256 floats.
All inputs are finite; a program needn't handle non-finite values.
Results may differ from a plain program's by a relative error of at most 0.0031.
Values may be sent and summed in bfloat16 or wider, within the bound.
A program may use at most 128 MiB of HBM per device.

v0:
```python
import math

import jax
import jax.numpy as jnp
from jax import lax
from jax.sharding import PartitionSpec as P

N = 8192
TILE = 128


HIGHEST = lax.Precision.HIGHEST


def twiddle_table(height, width, modulus, sign):
    product = (
        jnp.arange(height, dtype=jnp.int32)[:, None]
        * jnp.arange(width, dtype=jnp.int32)[None, :]
        % modulus
    )
    angle = sign * 2.0 * math.pi / modulus * product.astype(jnp.float32)
    return (jnp.cos(angle), jnp.sin(angle))


def complex_product(formula, real_part, imag_part, table_real, table_imag):
    first_real = jnp.einsum(formula, real_part, table_real, precision=HIGHEST)
    first_imag = jnp.einsum(formula, real_part, table_imag, precision=HIGHEST)
    return (
        first_real - jnp.einsum(formula, imag_part, table_imag, precision=HIGHEST),
        first_imag + jnp.einsum(formula, imag_part, table_real, precision=HIGHEST),
    )


def transform(real_part, imag_part, sign):
    length = real_part.shape[-1]
    inner_len = math.gcd(length, 64)
    outer_len = length // inner_len
    leading = real_part.shape[:-1]
    first_real, first_imag = twiddle_table(inner_len, inner_len, inner_len, sign)
    twist_real, twist_imag = twiddle_table(inner_len, outer_len, length, sign)
    second_real, second_imag = twiddle_table(outer_len, outer_len, outer_len, sign)
    shaped = leading + (inner_len, outer_len)
    imag_shaped = imag_part.reshape(shaped)
    section_real, section_imag = complex_product(
        "...ab,ak->...kb", real_part.reshape(shaped), imag_shaped, first_real, first_imag
    )
    turned_real = section_real * twist_real - section_imag * twist_imag
    turned_imag = section_real * twist_imag + section_imag * twist_real
    result_real, result_imag = complex_product(
        "...kb,bm->...mk", turned_real, turned_imag, second_real, second_imag
    )
    return (result_real.reshape(leading + (length,)), result_imag.reshape(leading + (length,)))


def to_pieces(values, pieces):
    height = values.shape[-2]
    length = values.shape[-1]
    leading = values.shape[:-2]
    width = length // pieces
    grid = values.reshape(leading + (height, pieces, width))
    return jnp.swapaxes(grid, -3, -1).reshape(leading + (width, pieces * height))


def mirrored(values):
    return jnp.roll(jnp.flip(values, -1), 1, -1)


def wavenumbers(index, length):
    signed = jnp.where(index < length // 2, index, index - length).astype(jnp.float32)
    wave = 2.0 * math.pi / length * signed
    slope = jnp.where(index == length // 2, 0.0, wave)
    return (wave, slope, (2.0 + jnp.cos(wave)) / 3.0)


def velocity_spectra(spec_real, spec_imag, col_index):
    col_wave, col_slope, col_prefilter = wavenumbers(col_index, N)
    row_wave, row_slope, row_prefilter = wavenumbers(jnp.arange(N, dtype=jnp.int32), N)
    kappa = math.pi / N
    factor = 1.0 / (
        (
            row_wave[None, :] * row_wave[None, :]
            + col_wave[:, None] * col_wave[:, None]
            + kappa * kappa
        )
        * (row_prefilter[None, :] * col_prefilter[:, None])
    )
    u_real = -(row_slope[None, :] * factor) * spec_imag
    u_imag = row_slope[None, :] * factor * spec_real
    v_real = col_slope[:, None] * factor * spec_imag
    v_imag = -(col_slope[:, None] * factor) * spec_real
    return (u_real, u_imag, v_real, v_imag)


def spline_weights(position):
    complement = 1.0 - position
    cubed = position * position * position
    return (
        complement * complement * complement / 6.0,
        (3.0 * cubed - 6.0 * position * position + 4.0) / 6.0,
        (-3.0 * cubed + 3.0 * position * position + 3.0 * position + 1.0) / 6.0,
        cubed / 6.0,
    )


def dense_weights(start, position, width):
    cells = jnp.arange(width, dtype=jnp.int32)
    overall_total = jnp.zeros(start.shape + (width,), jnp.float32)
    for offset, weight in enumerate(spline_weights(position)):
        overall_total = overall_total + jnp.where(
            cells == (start + offset)[..., None], weight[..., None], 0.0
        )
    return overall_total


def slot_velocity(chosen_tiles, cells, fractions):
    width = chosen_tiles.shape[-1]
    down = dense_weights(cells[:, 0] - 1, fractions[:, 0], width).astype(jnp.bfloat16)
    across = dense_weights(cells[:, 1] - 1, fractions[:, 1], width)
    inner = jnp.einsum("scr,sdrt->sdct", down, chosen_tiles, preferred_element_type=jnp.float32)
    return jnp.sum(inner * across[:, None], axis=-1)


def shards(vorticity, tile_list, float_slot, float_cell, float_frac):
    group_cols = lax.axis_size("gy")
    devices = lax.axis_size(("gx", "gy"))
    my_index = lax.axis_index(("gx", "gy"))
    block_rows, block_cols = vorticity.shape
    scale_back = 1.0 / (N * N)
    row_slab = lax.all_to_all(vorticity, "gy", split_axis=0, concat_axis=1, tiled=True)
    half_len = N // 2
    pairs = row_slab.reshape(row_slab.shape[0], half_len, 2)
    packed_real, packed_imag = transform(pairs[:, :, 0], pairs[:, :, 1], -1.0)
    mirror_real = mirrored(packed_real)
    mirror_imag = mirrored(packed_imag)
    even_real = (packed_real + mirror_real) * 0.5
    even_imag = (packed_imag - mirror_imag) * 0.5
    odd_real = (packed_imag + mirror_imag) * 0.5
    odd_imag = -(packed_real - mirror_real) * 0.5
    bins = jnp.arange(half_len, dtype=jnp.int32)
    angle = 2.0 * math.pi / N * bins.astype(jnp.float32)
    cosine = jnp.cos(angle)
    sine = jnp.sin(angle)
    first = bins == 0
    row_real = even_real + cosine * odd_real + sine * odd_imag
    row_imag = even_imag + cosine * odd_imag - sine * odd_real
    row_imag = jnp.where(first, even_real - odd_real, row_imag)
    sent_real, sent_imag = (
        lax.all_to_all(
            to_pieces(row_real, devices), ("gx", "gy"), split_axis=1, concat_axis=1, tiled=True
        ),
        lax.all_to_all(
            to_pieces(row_imag, devices), ("gx", "gy"), split_axis=1, concat_axis=1, tiled=True
        ),
    )
    spec_real, spec_imag = transform(sent_real, sent_imag, -1.0)
    half_cols = spec_real.shape[0]
    col_index = my_index * half_cols + jnp.arange(half_cols, dtype=jnp.int32)
    u_real, u_imag, v_real, v_imag = velocity_spectra(spec_real, spec_imag, col_index)
    edge_real = spec_real[0]
    edge_imag = spec_imag[0]
    flip_real = mirrored(edge_real)
    flip_imag = mirrored(edge_imag)
    ends_real = jnp.stack([(edge_real + flip_real) * 0.5, (edge_imag + flip_imag) * 0.5])
    ends_imag = jnp.stack([(edge_imag - flip_imag) * 0.5, -(edge_real - flip_real) * 0.5])
    end_index = jnp.array([0, N // 2], dtype=jnp.int32)
    eu_real, eu_imag, ev_real, ev_imag = velocity_spectra(ends_real, ends_imag, end_index)
    on_edge = jnp.logical_and(my_index == 0, jnp.arange(half_cols, dtype=jnp.int32) == 0)[:, None]
    u_real = jnp.where(on_edge, (eu_real[0] - eu_imag[1])[None, :], u_real)
    u_imag = jnp.where(on_edge, (eu_imag[0] + eu_real[1])[None, :], u_imag)
    v_real = jnp.where(on_edge, (ev_real[0] - ev_imag[1])[None, :], v_real)
    v_imag = jnp.where(on_edge, (ev_imag[0] + ev_real[1])[None, :], v_imag)
    both_real, both_imag = transform(jnp.stack([u_real, v_real]), jnp.stack([u_imag, v_imag]), 1.0)
    back_real, back_imag = (
        lax.all_to_all(
            to_pieces(both_real, devices), ("gx", "gy"), split_axis=2, concat_axis=2, tiled=True
        ),
        lax.all_to_all(
            to_pieces(both_imag, devices), ("gx", "gy"), split_axis=2, concat_axis=2, tiled=True
        ),
    )
    flip_back_real = mirrored(back_real)
    flip_back_imag = mirrored(back_imag)
    nyquist = back_imag[..., 0:1]
    low_imag = jnp.where(first, 0.0, back_imag)
    high_real = jnp.where(first, nyquist, flip_back_real)
    high_imag = jnp.where(first, 0.0, -flip_back_imag)
    sum_real = back_real + high_real
    sum_imag = low_imag + high_imag
    diff_real = back_real - high_real
    diff_imag = low_imag - high_imag
    turn_real = diff_real * cosine - diff_imag * sine
    turn_imag = diff_real * sine + diff_imag * cosine
    rows_even, rows_odd = transform(sum_real - turn_imag, sum_imag + turn_real, 1.0)
    fields = jnp.stack([rows_even, rows_odd], axis=-1).reshape(rows_even.shape[:-1] + (N,))
    coeffs = fields * scale_back
    coeff_block = lax.all_to_all(
        coeffs.astype(jnp.bfloat16), "gy", split_axis=2, concat_axis=1, tiled=True
    )
    tile_rows = block_rows // TILE
    tile_cols = block_cols // TILE
    tiles = coeff_block.reshape(2, tile_rows, TILE, tile_cols, TILE).transpose(1, 3, 0, 2, 4)
    tiles = tiles.reshape(tile_rows * tile_cols, 2, TILE, TILE)
    wanted = tile_list[0]
    tile_count = wanted.shape[0]
    per_row = N // TILE
    grid_row = wanted // per_row
    grid_col = wanted % per_row
    owner_index = grid_row // tile_rows * group_cols + grid_col // tile_cols
    local_index = grid_row % tile_rows * tile_cols + grid_col % tile_cols
    float_total = float_slot.shape[0]
    capacity = 2 * float_total // tile_count
    member = (float_slot[:, None] == jnp.arange(tile_count, dtype=jnp.int32)[None, :]).astype(
        jnp.int32
    )
    slot_rank = jnp.sum((jnp.cumsum(member, axis=0) - member) * member, axis=1)
    placing = float_slot * capacity + slot_rank
    grouped_cell = jnp.zeros((2, tile_count * capacity), jnp.int32).at[:, placing].set(float_cell)
    grouped_cell = grouped_cell.reshape(2, tile_count, capacity).transpose(1, 0, 2)
    grouped_frac = jnp.zeros((2, tile_count * capacity), jnp.float32).at[:, placing].set(float_frac)
    grouped_frac = grouped_frac.reshape(2, tile_count, capacity).transpose(1, 0, 2)
    owns = (owner_index[:, None] == jnp.arange(devices, dtype=jnp.int32)[None, :]).astype(jnp.int32)
    request = jnp.sum(owns * (local_index[:, None] + 1), axis=0) - 1
    request = lax.all_to_all(request, ("gx", "gy"), split_axis=0, concat_axis=0, tiled=True)
    outgoing = jnp.take(tiles, jnp.maximum(request, 0), axis=0)
    incoming = lax.all_to_all(outgoing, ("gx", "gy"), split_axis=0, concat_axis=0, tiled=True)
    grouped = slot_velocity(jnp.take(incoming, owner_index, axis=0), grouped_cell, grouped_frac)
    flattened = grouped.transpose(1, 0, 2).reshape(2, tile_count * capacity)
    return jnp.take(flattened, placing, axis=1)


def solution(mesh):
    in_specs = (
        P("gx", "gy"),
        P(("gx", "gy"), None),
        P(("gx", "gy")),
        P(None, ("gx", "gy")),
        P(None, ("gx", "gy")),
    )
    out_specs = P(None, ("gx", "gy"))
    return jax.shard_map(shards, mesh=mesh, in_specs=in_specs, out_specs=out_specs, check_vma=False)
```

profile of v0, /device:TPU:0, one launch (start us, length us, event | category | flops | bytes accessed | tf_op | source)
XLA Modules:
  0.0 1528.8 jit_solution(12083783068196865392)
XLA Ops:
  14.6 94.4 %all-to-all-done.1 = f32[8,256,1024]{1,2,0:T(8,128)} async-done(((f32[8,256,1024]{1,2,0:T(8,128)}), f32[8,256,1024]{1,2,0:T(8,128)}, u32[]{:S(2)}, u32[]{:S(2)}) %all-to-all-start.1) | async-done | bytes 8388640 | tf_op jit(solution)/shard_map/all_to_all | solution.py:129
  195.0 33.6 %slice.129 = f32[256,4095]{0,1:T(8,128)} reverse(f32[256,4095]{0,1:T(8,128)} %slice.170), dimensions={1} | reverse | bytes 8386560 | tf_op jit(solution)/shard_map/jit(_roll_static)/slice | solution.py:65
  228.6 33.6 %slice.132 = f32[256,4095]{0,1:T(8,128)} reverse(f32[256,4095]{0,1:T(8,128)} %slice.172), dimensions={1} | reverse | bytes 8386560 | tf_op jit(solution)/shard_map/jit(_roll_static)/slice | solution.py:65
  274.3 98.2 %all_to_all.64 = f32[128,32,256]{2,0,1:T(8,128)} all-to-all(f32[128,32,256]{2,0,1:T(8,128)S(1)} %get-tuple-element.18), channel_id=1, replica_groups=mesh['gx'=4,'gy'=8] {'gx','gy'}, dimensions={1} | all-to-all | bytes 8388608 | tf_op jit(solution)/shard_map/all_to_all | solution.py:148
  402.2 68.0 %all-to-all-done.3 = f32[128,32,256]{2,0,1:T(8,128)} async-done(((f32[128,32,256]{2,0,1:T(8,128)}), f32[128,32,256]{2,0,1:T(8,128)}, u32[]{:S(2)}, u32[]{:S(2)}) %all-to-all-start.3) | async-done | bytes 4194336 | tf_op jit(solution)/shard_map/all_to_all | solution.py:151
  595.1 19.7 %subtract_bitcast_fusion.3 = (f32[2,128,64,128]{3,2,1,0:T(8,128)}, f32[2,128,64,128]{3,2,1,0:T(8,128)}) fusion(f32[64,128]{1,0:T(8,128)S(1)} %get-tuple-element.75, f32[64,128]{1,0:T(8,128)S(1)} %get-tuple-element.76, f32[64,2,128,128]{3,0,2,1:T(8,128)} %fusion.28, f32[64,2,128,128]{3,0,2,1:T(8,128)} %fusion.26, f32[64,2,128,128]{3,0,2,1:T(8,128)} %fusion.27, ...), kind=kOutput, calls=%fused_computation.21 | convolution fusion | flops 1629544448 | bytes 50397184 | tf_op jit(solution)/shard_map/...ab,ak->...kb/dot_general | solution.py:26
  614.7 15.8 %fusion.18 = f32[128,2,128,64]{2,0,3,1:T(8,128)S(1)} fusion(f32[2,128,64,128]{3,2,1,0:T(8,128)} %get-tuple-element.14), kind=kOutput, calls=%fused_computation.38 | convolution fusion | flops 3221454848 | bytes 16777216 | tf_op jit(solution)/shard_map/...kb,bm->...mk/dot_general | solution.py:30
  659.6 15.4 %copy.259 = f32[2,256,4096]{1,0,2:T(2,128)} copy(f32[2,256,4096]{1,2,0:T(8,128)} %bitcast.355) | data formatting | bytes 16777216 | tf_op jit(solution)/shard_map/reshape | solution.py:61
  679.3 15.4 %fusion.20 = f32[128,2,128,64]{2,0,3,1:T(8,128)S(1)} fusion(f32[2,128,64,128]{3,2,1,0:T(8,128)} %get-tuple-element.14), kind=kOutput, calls=%fused_computation.40 | convolution fusion | flops 3221454848 | bytes 16777216 | tf_op jit(solution)/shard_map/...kb,bm->...mk/dot_general | solution.py:29
  694.7 15.7 %subtract_bitcast_fusion.2 = f32[2,128,128,64]{1,2,3,0:T(8,128)S(1)} fusion(f32[128,2,128,64]{2,0,3,1:T(8,128)S(1)} %fusion.20, f32[2,128,64,128]{3,2,1,0:T(8,128)} %get-tuple-element.13), kind=kOutput, calls=%fused_computation.19 | convolution fusion | flops 3223552000 | bytes 25165824 | tf_op jit(solution)/shard_map/...kb,bm->...mk/dot_general | solution.py:26
  727.6 15.4 %copy.254 = f32[2,256,4096]{1,0,2:T(2,128)} copy(f32[2,256,4096]{1,2,0:T(8,128)} %bitcast.357) | data formatting | bytes 16777216 | tf_op jit(solution)/shard_map/reshape | solution.py:61
  743.0 122.2 %all-to-all-done.5 = f32[2,256,4096]{1,0,2:T(2,128)} async-done(((f32[2,256,4096]{1,0,2:T(2,128)}), f32[2,256,4096]{1,0,2:T(2,128)}, u32[]{:S(2)}, u32[]{:S(2)}) %all-to-all-start.5) | async-done | bytes 8388640 | tf_op jit(solution)/shard_map/all_to_all | solution.py:177
  879.3 66.3 %slice.154 = f32[2,256,4095]{1,2,0:T(8,128)} reverse(f32[2,256,4095]{1,2,0:T(8,128)} %copy.375), dimensions={2} | reverse | bytes 16773120 | tf_op jit(solution)/shard_map/jit(_roll_static)/slice | solution.py:65
  946.3 108.7 %all-to-all-done.4 = f32[2,256,4096]{1,0,2:T(2,128)} async-done(((f32[2,256,4096]{1,0,2:T(2,128)}), f32[2,256,4096]{1,0,2:T(2,128)}, u32[]{:S(2)}, u32[]{:S(2)}) %all-to-all-start.4) | async-done | bytes 8388640 | tf_op jit(solution)/shard_map/all_to_all | solution.py:174
  1066.8 66.3 %slice.152 = f32[2,256,4095]{1,2,0:T(8,128)} reverse(f32[2,256,4095]{1,2,0:T(8,128)} %copy.373), dimensions={2} | reverse | bytes 16773120 | tf_op jit(solution)/shard_map/jit(_roll_static)/slice | solution.py:65
  1159.1 13.6 fusion.12
  1185.9 24.8 %subtract_bitcast_fusion.1 = (f32[2,256,64,64]{1,2,3,0:T(8,128)}, f32[2,256,64,64]{1,2,3,0:T(8,128)}) fusion(f32[64,64]{0,1:T(8,128)S(1)} %get-tuple-element.79, f32[64,64]{0,1:T(8,128)S(1)} %get-tuple-element.80, f32[64,2,256,64]{2,0,3,1:T(8,128)} %fusion.14, f32[64,2,256,64]{2,0,3,1:T(8,128)} %fusion.10, f32[64,2,256,64]{2,0,3,1:T(8,128)} %fusion.12, ...), kind=kOutput, calls=%fused_computation.15 | convolution fusion | flops 1627447296 | bytes 50364416 | tf_op jit(solution)/shard_map/...ab,ak->...kb/dot_general | solution.py:26
  1210.7 18.0 %fusion.4 = f32[64,2,256,64]{2,0,3,1:T(8,128)} fusion(f32[2,256,64,64]{1,2,3,0:T(8,128)} %get-tuple-element.12), kind=kOutput, calls=%fused_computation.24 | convolution fusion | flops 1610670080 | bytes 16777216 | tf_op jit(solution)/shard_map/...kb,bm->...mk/dot_general | solution.py:29
  1241.5 15.5 %subtract_bitcast_fusion = f32[2,256,64,64]{1,2,3,0:T(8,128)} fusion(f32[64,2,256,64]{2,0,3,1:T(8,128)} %fusion.4, f32[2,256,64,64]{1,2,3,0:T(8,128)S(1)} %bitcast.334), kind=kOutput, calls=%fused_computation.13 | convolution fusion | flops 1612767232 | bytes 25165824 | tf_op jit(solution)/shard_map/...kb,bm->...mk/dot_general | solution.py:26
  1268.5 13.6 add_bitcast_fusion
  1294.8 16.4 %copy.277 = bf16[2,256,4096,2]{1,0,3,2:T(2,128)(2,1)} copy(bf16[2,256,4096,2]{1,2,0,3:T(8,128)(2,1)} %fusion) | data formatting | bytes 16777216 | tf_op jit(solution)/shard_map/convert_element_type | solution.py:197
  1317.9 92.7 %all-to-all-done.6 = bf16[2,256,8192]{1,0,2:T(2,128)(2,1)} async-done(((bf16[2,256,8192]{1,0,2:T(2,128)(2,1)}), bf16[2,256,8192]{1,0,2:T(2,128)(2,1)}, u32[]{:S(2)}, u32[]{:S(2)}) %all-to-all-start.6) | async-done | bytes 8388640 | tf_op jit(solution)/shard_map/all_to_all | solution.py:196
  1410.6 21.0 %copy.278 = bf16[2,256,8,1024]{3,1,2,0:T(8,128)(2,1)} copy(bf16[2,256,8,1024]{1,0,3,2:T(2,128)(2,1)} %bitcast.67) | data formatting | bytes 16777216 | tf_op jit(solution)/shard_map/all_to_all | solution.py:196
  1486.0 22.5 %all-to-all-done.7 = bf16[32,2,128,128]{3,2,1,0:T(8,128)(2,1)} async-done(((bf16[32,2,128,128]{3,2,1,0:T(8,128)(2,1)}), bf16[32,2,128,128]{3,2,1,0:T(8,128)(2,1)}, u32[]{:S(2)}, u32[]{:S(2)}) %all-to-all-start.7) | async-done | bytes 2097184 | tf_op jit(solution)/shard_map/all_to_all | solution.py:225
  (195 shorter events, 501.2 us)
Async XLA Ops:
  9.1 99.8 %all-to-all-start.1 = ((f32[8,256,1024]{1,2,0:T(8,128)}), f32[8,256,1024]{1,2,0:T(8,128)}, u32[]{:S(2)}, u32[]{:S(2)}) async-start(f32[8,256,1024]{1,2,0:T(8,128)} %copy.221), calls=%async_computation.1 | async-start | bytes 16777216 | tf_op jit(solution)/shard_map/all_to_all | solution.py:129
  372.5 97.7 %all-to-all-start.3 = ((f32[128,32,256]{2,0,1:T(8,128)}), f32[128,32,256]{2,0,1:T(8,128)}, u32[]{:S(2)}, u32[]{:S(2)}) async-start(f32[128,32,256]{2,0,1:T(8,128)} %get-tuple-element.17), calls=%async_computation.3 | async-start | bytes 8388608 | tf_op jit(solution)/shard_map/all_to_all | solution.py:151
  388.5 8.2 copy-start.14
  481.7 8.0 copy-start.9
  481.8 8.0 copy-start.16
  495.2 6.7 copy-start.12
  495.2 6.7 copy-start.7
  517.1 8.6 copy-start.8
  565.7 19.7 %copy-start.10 = (f32[1,128,64,128]{3,2,1,0:T(8,128)}, f32[1,128,64,128]{3,2,1,0:T(8,128)S(1)}, u32[]{:S(2)}) copy-start(f32[1,128,64,128]{3,2,1,0:T(8,128)S(1)} %get-tuple-element.27) | copy-start | bytes 12582916
  565.7 19.7 %copy-start.11 = (f32[1,128,64,128]{3,2,1,0:T(8,128)}, f32[1,128,64,128]{3,2,1,0:T(8,128)S(1)}, u32[]{:S(2)}) copy-start(f32[1,128,64,128]{3,2,1,0:T(8,128)S(1)} %get-tuple-element.28) | copy-start | bytes 12582916
  614.7 15.8 %copy-start = (f32[2,128,64,128]{3,2,1,0:T(8,128)S(1)}, f32[2,128,64,128]{3,2,1,0:T(8,128)}, u32[]{:S(2)}) copy-start(f32[2,128,64,128]{3,2,1,0:T(8,128)} %get-tuple-element.13) | copy-start | bytes 25165828
  675.0 190.2 %all-to-all-start.5 = ((f32[2,256,4096]{1,0,2:T(2,128)}), f32[2,256,4096]{1,0,2:T(2,128)}, u32[]{:S(2)}, u32[]{:S(2)}) async-start(f32[2,256,4096]{1,0,2:T(2,128)} %copy.259), calls=%async_computation.5 | async-start | bytes 16777216 | tf_op jit(solution)/shard_map/all_to_all | solution.py:177
  743.0 125.9 %copy-start.21 = (s32[1,16]{1,0:T(1,128)S(1)}, s32[1,16]{1,0:T(1,128)}, u32[]{:S(2)}) copy-start(s32[1,16]{1,0:T(1,128)} %param.7) | copy-start | bytes 196
  865.2 189.8 %all-to-all-start.4 = ((f32[2,256,4096]{1,0,2:T(2,128)}), f32[2,256,4096]{1,0,2:T(2,128)}, u32[]{:S(2)}, u32[]{:S(2)}) async-start(f32[2,256,4096]{1,0,2:T(2,128)} %copy.254), calls=%async_computation.4 | async-start | bytes 16777216 | tf_op jit(solution)/shard_map/all_to_all | solution.py:174
  1054.9 256.3 %all-to-all-start = ((s32[32,1,1]{2,1,0:T(1,128)}), s32[32,1,1]{2,1,0:T(1,128)S(1)}, u32[]{:S(2)}, u32[]{:S(2)}) async-start(s32[32,1,1]{2,1,0:T(1,128)} %copy.220), calls=%async_computation | async-start | bytes 32768 | tf_op jit(solution)/shard_map/all_to_all | solution.py:223
  1145.9 26.8 %copy-start.2 = (f32[2,256,4096]{1,2,0:T(8,128)}, f32[2,256,4096]{1,2,0:T(8,128)S(1)}, u32[]{:S(2)}) copy-start(f32[2,256,4096]{1,2,0:T(8,128)S(1)} %get-tuple-element.16) | copy-start | bytes 25165828
  1210.7 18.0 %copy-start.1 = (f32[2,256,64,64]{1,2,3,0:T(8,128)S(1)}, f32[2,256,64,64]{1,2,3,0:T(8,128)}, u32[]{:S(2)}) copy-start(f32[2,256,64,64]{1,2,3,0:T(8,128)} %get-tuple-element.12) | copy-start | bytes 25165828
  1210.7 30.7 %slice-start = ((s8[8388608]{0:T(1024)(128)(4,1)}), s8[4194304]{0:T(1024)(128)(4,1)S(1)}, s32[]{:S(2)}) async-start(s8[8388608]{0:T(1024)(128)(4,1)} %bitcast.333), calls=%async_computation.8 | async-start | bytes 8388608
  1228.8 12.7 slice-start.1
  1282.0 8.4 copy-start.15
  1311.2 99.4 %all-to-all-start.6 = ((bf16[2,256,8192]{1,0,2:T(2,128)(2,1)}), bf16[2,256,8192]{1,0,2:T(2,128)(2,1)}, u32[]{:S(2)}, u32[]{:S(2)}) async-start(bf16[2,256,8192]{1,0,2:T(2,128)(2,1)} %bitcast.353), calls=%async_computation.6 | async-start | bytes 16777216 | tf_op jit(solution)/shard_map/all_to_all | solution.py:196
  1454.0 11.0 copy-start.19
  1455.6 52.9 %all-to-all-start.7 = ((bf16[32,2,128,128]{3,2,1,0:T(8,128)(2,1)}), bf16[32,2,128,128]{3,2,1,0:T(8,128)(2,1)}, u32[]{:S(2)}, u32[]{:S(2)}) async-start(bf16[32,2,128,128]{3,2,1,0:T(8,128)(2,1)} %broadcast_select_fusion), calls=%async_computation.7 | async-start | bytes 4194304 | tf_op jit(solution)/shard_map/all_to_all | solution.py:225
  1459.8 12.5 copy-start.20
  (7 other events, 25.9 us)
where the time goes:
time: 1550 us; the launch traced here: 1530 us
  waiting for transfers between devices  508 us (33%)
  local copies, waits for them, and re-layouts  492 us (32%)
  matrix products  353 us (23%)
  blocking collectives  98.2 us (6%)
  other arithmetic  47.2 us (3%)
  starting transfers between devices  29.2 us (2%)
    slice x15, local copies, waits for them, and re-layouts, mirrored(): return jnp.roll(jnp.flip(values, -1), 1, -1)  217 us
    all_to_all x1, waiting for transfers between devices, shards(): lax.all_to_all(to_pieces(both_imag, devices), ('gx', 'gy'), split_axis=2,...  122 us
    all_to_all x1, waiting for transfers between devices, shards(): lax.all_to_all(to_pieces(both_real, devices), ('gx', 'gy'), split_axis=2,...  109 us
    dot_general x8, matrix products, complex_product(): first_real = jnp.einsum(formula, real_part, table_real, precision=HIGHEST)  100 us
    all_to_all x1, blocking collectives, shards(): lax.all_to_all(to_pieces(row_real, devices), ('gx', 'gy'), split_axis=1,...  98.2 us
    all_to_all x1, waiting for transfers between devices, shards(): lax.all_to_all(vorticity, 'gy', split_axis=0, concat_axis=1, tiled=True)  94.4 us
    all_to_all x1, waiting for transfers between devices, shards(): lax.all_to_all(coeffs.astype(jnp.bfloat16), 'gy', split_axis=2, concat_ax...  92.7 us
    dot_general x8, matrix products, complex_product(): jnp.einsum(formula, imag_part, table_real, precision=HIGHEST)  81.4 us
  transfers between devices with their start and end apart: 7, of which 6 were waited for; matrix products, arithmetic and copies ran while one was open for 29% of the time, Pallas kernels for 0%

commit v1 on v0

v1 whole, which is shorter than its diff:
```python
import math

import jax
import jax.numpy as jnp
import numpy as np
from jax import lax
from jax.sharding import PartitionSpec as P

TILE = 128
HIGH = lax.Precision.HIGH
F32 = jnp.float32
BF16 = jnp.bfloat16
F16 = jnp.float16


def root(height, width, modulus, sign):
    product = np.arange(height)[:, None] * np.arange(width)[None, :] % modulus
    angle = sign * 2.0 * math.pi / modulus * product
    return np.cos(angle), np.sin(angle)


def mixing(height, width, modulus, sign):
    real, imag = root(height, width, modulus, sign)
    return np.stack([np.stack([real, imag], 1), np.stack([-imag, real], 1)]).astype(np.float32)


def twiddle_table(height, width, modulus, sign):
    product = (
        jnp.arange(height, dtype=jnp.int32)[:, None]
        * jnp.arange(width, dtype=jnp.int32)[None, :]
        % modulus
    )
    angle = sign * 2.0 * math.pi / modulus * product.astype(F32)
    return jnp.cos(angle), jnp.sin(angle)


def dot(formula, left, right):
    return jnp.einsum(formula, left, right, precision=HIGH, preferred_element_type=F32)


def turned(values, table, axis_shape):
    real, imag = (part.reshape(axis_shape) for part in table)
    return jnp.stack(
        [values[0] * real - values[1] * imag, values[0] * imag + values[1] * real]
    )


def mirrored(values):
    return jnp.roll(jnp.flip(values, -1), 1, -1)


def wavenumbers(index, length):
    signed = jnp.where(index < length // 2, index, index - length).astype(F32)
    wave = 2.0 * math.pi / length * signed
    slope = jnp.where(index == length // 2, 0.0, wave)
    return (wave, slope, (2.0 + jnp.cos(wave)) / 3.0)


def multipliers(row_index, col_index, length):
    row_wave, row_slope, row_prefilter = wavenumbers(row_index, length)
    col_wave, col_slope, col_prefilter = wavenumbers(col_index, length)
    kappa = math.pi / length
    factor = 1.0 / (
        (row_wave * row_wave + col_wave * col_wave + kappa * kappa)
        * (row_prefilter * col_prefilter)
    )
    return row_slope * factor, col_slope * factor


def spline_weights(position):
    complement = 1.0 - position
    cubed = position * position * position
    return (
        complement * complement * complement / 6.0,
        (3.0 * cubed - 6.0 * position * position + 4.0) / 6.0,
        (-3.0 * cubed + 3.0 * position * position + 3.0 * position + 1.0) / 6.0,
        cubed / 6.0,
    )


def dense_weights(start, position, width):
    cells = jnp.arange(width, dtype=jnp.int32)
    overall_total = jnp.zeros(start.shape + (width,), F32)
    for offset, weight in enumerate(spline_weights(position)):
        overall_total = overall_total + jnp.where(
            cells == (start + offset)[..., None], weight[..., None], 0.0
        )
    return overall_total


def slot_velocity(chosen_tiles, cells, fractions):
    width = chosen_tiles.shape[-1]
    down = dense_weights(cells[:, 0] - 1, fractions[:, 0], width).astype(BF16)
    across = dense_weights(cells[:, 1] - 1, fractions[:, 1], width)
    inner = jnp.einsum("scr,sdtr->sdct", down, chosen_tiles, preferred_element_type=F32)
    return jnp.sum(inner * across[:, None], axis=-1)


def shards(vorticity, tile_list, float_slot, float_cell, float_frac):
    both = ("gx", "gy")
    group_cols = lax.axis_size("gy")
    devices = lax.axis_size(both)
    my_index = lax.axis_index(both)
    block_rows, block_cols = vorticity.shape
    length = block_cols * group_cols
    rows = length // devices
    cols = length // 2 // devices
    low = TILE
    high = length // low
    half_low = low // 2
    alternating = jnp.asarray(1.0 - 2.0 * (np.arange(low) % 2), F32)

    slab = vorticity.astype(F16).reshape(group_cols, rows, block_cols)
    slab = lax.all_to_all(slab, "gy", split_axis=0, concat_axis=0)
    slab = slab.reshape(group_cols, rows, block_cols // low, low)
    real, imag = root(high, high, high, -1.0)
    table = np.stack([real, imag], 1).reshape(group_cols, block_cols // low, 2, high)
    first = dot("hgck,hrgb->ckrb", table.astype(np.float32), slab.astype(F32))
    twist = twiddle_table(high, low, length, -1.0)
    nyquist = jnp.sum(first[0, 0] * alternating[None, :], axis=-1)
    first = turned(first, twist, (high, 1, low))
    spec = dot("cbdm,ckrb->dmkr", mixing(low, half_low, low, -1.0), first)
    here = jnp.logical_and(
        jnp.arange(half_low)[:, None] == 0, jnp.arange(high)[None, :] == 0
    )[:, :, None]
    spec = jnp.stack([spec[0], jnp.where(here, nyquist[None, None, :], spec[1])])
    sent = (spec * 0.125).reshape(2, devices, cols, rows).astype(F16)
    sent = lax.all_to_all(sent, both, split_axis=1, concat_axis=0)

    if rows % low == 0:
        got = sent.reshape(devices, 2, cols, rows // low, low)
        table = mixing(high, high, high, -1.0).reshape(2, devices, rows // low, 2, high)
        second = dot("csgdk,scngb->dknb", table, got.astype(F32) * 8.0)
    else:
        got = sent.reshape(high, low // rows, 2, cols, rows).transpose(0, 2, 3, 1, 4)
        got = got.reshape(high, 2, cols, low)
        second = dot("cadk,acnb->dknb", mixing(high, high, high, -1.0), got.astype(F32) * 8.0)
    second = turned(second, twist, (high, 1, low))
    full = dot("cbdm,cknb->dknm", mixing(low, low, low, -1.0), second)

    row_index = (
        jnp.arange(high, dtype=jnp.int32)[:, None, None]
        + high * jnp.arange(low, dtype=jnp.int32)[None, None, :]
    )
    col_index = (my_index * cols + jnp.arange(cols, dtype=jnp.int32))[None, :, None]
    row_gain, col_gain = multipliers(row_index, col_index, length)
    row_gain = row_gain * 2.0
    col_gain = col_gain * 2.0
    u_real, u_imag = -row_gain * full[1], row_gain * full[0]
    v_real, v_imag = col_gain * full[1], -col_gain * full[0]

    edge_real = full[0, :, 0].T.reshape(length)
    edge_imag = full[1, :, 0].T.reshape(length)
    flip_real = mirrored(edge_real)
    flip_imag = mirrored(edge_imag)
    ends_real = jnp.stack([(edge_real + flip_real) * 0.5, (edge_imag + flip_imag) * 0.5])
    ends_imag = jnp.stack([(edge_imag - flip_imag) * 0.5, -(edge_real - flip_real) * 0.5])
    end_row, end_col = multipliers(
        jnp.arange(length, dtype=jnp.int32)[None, :],
        jnp.array([0, length // 2], dtype=jnp.int32)[:, None],
        length,
    )
    eu_real, eu_imag = -end_row * ends_imag, end_row * ends_real
    ev_real, ev_imag = end_col * ends_imag, -end_col * ends_real
    on_edge = jnp.logical_and(my_index == 0, jnp.arange(cols) == 0)[None, :, None]

    def place(edge, values):
        return jnp.where(on_edge, edge.reshape(low, high).T[:, None, :], values)

    fields = jnp.stack(
        [
            jnp.stack([place(eu_real[0] - eu_imag[1], u_real), place(ev_real[0] - ev_imag[1], v_real)]),
            jnp.stack([place(eu_imag[0] + eu_real[1], u_imag), place(ev_imag[0] + ev_real[1], v_imag)]),
        ]
    )

    third = dot("cmdb,cfknm->dfknb", mixing(low, low, low, 1.0), fields)
    untwist = twiddle_table(high, low, length, 1.0)
    third = turned(third, untwist, (1, high, 1, low))
    back = dot("ckda,cfknb->adfnb", mixing(high, high, high, 1.0), third)
    back = back.astype(BF16)
    if rows % low == 0:
        back = back.reshape(devices, rows // low, 2, 2, cols, low)
    else:
        back = back.reshape(high, 2, 2, cols, low // rows, rows).transpose(0, 4, 1, 2, 3, 5)
        back = back.reshape(devices, 1, 2, 2, cols, rows)
    back = lax.all_to_all(back, both, split_axis=0, concat_axis=0)

    groups, lanes = back.shape[1], back.shape[-1]
    if cols % high == 0:
        back = back.reshape(devices * groups, 2, 2, cols // high, high, lanes)
        back = back.reshape(devices, groups, 2, 2, cols // high, high, lanes)
        table = mixing(half_low, low, low, 1.0).reshape(2, devices, cols // high, 2, low)
        fourth = dot("csmdb,sgcfmky->dgfkby", table, back.astype(F32))
        nyquist = back[0, :, 1, :, 0, 0]
    else:
        back = back.reshape(half_low, high // cols, groups, 2, 2, cols, lanes)
        back = back.transpose(0, 2, 3, 4, 1, 5, 6).reshape(half_low, groups, 2, 2, high, lanes)
        fourth = dot("cmdb,mgcfky->dgfkby", mixing(half_low, low, low, 1.0), back.astype(F32))
        nyquist = back[0, :, 1, :, 0]
    lift = nyquist.astype(F32)[:, :, None, None, :] * alternating[None, None, None, :, None]
    first_k = (jnp.arange(high) == 0)[None, None, :, None, None]
    fourth = jnp.stack([fourth[0] + jnp.where(first_k, lift, 0.0), fourth[1]])
    fourth = turned(fourth, untwist, (1, 1, high, low, 1))
    real, imag = root(high, high, high, 1.0)
    table = np.stack([real, -imag]).astype(np.float32) / (length * length)
    coeffs = dot("cka,cgfkby->agfby", table, fourth).astype(BF16)
    tile_rows = block_rows // TILE
    tile_cols = block_cols // TILE
    coeffs = coeffs.reshape(group_cols, tile_cols * groups, 2, TILE, lanes)
    tiles = lax.all_to_all(coeffs, "gy", split_axis=0, concat_axis=0)
    if lanes == TILE:
        tiles = tiles.reshape(group_cols, tile_cols, groups, 2, TILE, TILE)
        tile_groups = groups
    else:
        parts = TILE // lanes
        tiles = tiles.reshape(group_cols // parts, parts, tile_cols, 2, TILE, lanes)
        tiles = tiles.transpose(0, 2, 3, 4, 1, 5)
        tile_groups = 1
    tiles = tiles.reshape(tile_rows * tile_cols, 2, TILE, TILE)

    wanted = tile_list[0]
    tile_count = wanted.shape[0]
    per_row = length // TILE
    grid_row = wanted // per_row
    grid_col = wanted % per_row
    owner_index = grid_row // tile_rows * group_cols + grid_col // tile_cols
    local_row = grid_row % tile_rows
    local_index = (
        local_row // tile_groups * tile_cols + grid_col % tile_cols
    ) * tile_groups + local_row % tile_groups
    float_total = float_slot.shape[0]
    capacity = 2 * float_total // tile_count
    member = (float_slot[:, None] == jnp.arange(tile_count, dtype=jnp.int32)[None, :]).astype(
        jnp.int32
    )
    slot_rank = jnp.sum((jnp.cumsum(member, axis=0) - member) * member, axis=1)
    placing = float_slot * capacity + slot_rank
    grouped_cell = jnp.zeros((2, tile_count * capacity), jnp.int32).at[:, placing].set(float_cell)
    grouped_cell = grouped_cell.reshape(2, tile_count, capacity).transpose(1, 0, 2)
    grouped_frac = jnp.zeros((2, tile_count * capacity), F32).at[:, placing].set(float_frac)
    grouped_frac = grouped_frac.reshape(2, tile_count, capacity).transpose(1, 0, 2)
    owns = (owner_index[:, None] == jnp.arange(devices, dtype=jnp.int32)[None, :]).astype(jnp.int32)
    request = jnp.sum(owns * (local_index[:, None] + 1), axis=0) - 1
    request = lax.all_to_all(request, both, split_axis=0, concat_axis=0, tiled=True)
    outgoing = jnp.take(tiles, jnp.maximum(request, 0), axis=0)
    incoming = lax.all_to_all(outgoing, both, split_axis=0, concat_axis=0, tiled=True)
    grouped = slot_velocity(jnp.take(incoming, owner_index, axis=0), grouped_cell, grouped_frac)
    flattened = grouped.transpose(1, 0, 2).reshape(2, tile_count * capacity)
    return jnp.take(flattened, placing, axis=1)


def solution(mesh):
    in_specs = (
        P("gx", "gy"),
        P(("gx", "gy"), None),
        P(("gx", "gy")),
        P(None, ("gx", "gy")),
        P(None, ("gx", "gy")),
    )
    out_specs = P(None, ("gx", "gy"))
    return jax.shard_map(shards, mesh=mesh, in_specs=in_specs, out_specs=out_specs, check_vma=False)
```

time: 1550 us -> 875 us (0.56)
  local copies, waits for them, and re-layouts: 492 us -> 137 us
  matrix products: 353 us -> 141 us
  blocking collectives: 98.2 us -> 0 us
  other arithmetic: 47.2 us -> 119 us
  waiting for transfers between devices: 508 us -> 442 us
    slice x15 -> x4, local copies, waits for them, and re-layouts: 217 us -> 1.24 us  [mirrored(): return jnp.roll(jnp.flip(values, -1), 1, -1)]
    dot_general x33 -> x9, matrix products: 353 us -> 141 us  [the longest x8 132 us: dot(): jnp.einsum(formula, left, right, precision=HIGH, preferred_element_type=F32)]
    all_to_all x1 -> x0, blocking collectives: 98.2 us -> none  [shards(): lax.all_to_all(to_pieces(row_real, devices), ('gx', 'gy'), split_axis=1,...]
    all_to_all x7 -> x6, waiting for transfers between devices: 508 us -> 442 us  [the longest x1 185 us: shards(): back = lax.all_to_all(back, both, split_axis=0, concat_axis=0)]
    another operation x3 -> x9, other arithmetic: 4.81 us -> 50.9 us  [the longest x4 38 us: turned(): jnp.stack([values[0] * real - values[1] * imag, values[0] * imag + values...]
    reshape x7 -> x6, local copies, waits for them, and re-layouts: 61.8 us -> 23.8 us  [the longest x1 16.3 us: shards(): back = back.reshape(devices, rows // low, 2, 2, cols, low)]
    sub x1 -> x7, other arithmetic: 0.02 us -> 34 us  [the longest x4 33.6 us: turned(): values[0] * real - values[1] * imag]
    another operation x1 -> x2, local copies, waits for them, and re-layouts: 0.43 us -> 32.6 us  [the longest x1 32.1 us: turned(): jnp.stack([values[0] * real - values[1] * imag, values[0] * imag + values...]
  transfers between devices with their start and end apart: 7 -> 6, of which waited for: 6 -> 5; matrix products, arithmetic and copies ran while one was open for 29% -> 18% of each run, Pallas kernels for 0% -> 0%
where the time goes in v1:
time: 875 us; the launch traced here: 867 us
  waiting for transfers between devices  442 us (51%)
  matrix products  141 us (16%)
  local copies, waits for them, and re-layouts  137 us (16%)
  other arithmetic  119 us (14%)
  starting transfers between devices  26.5 us (3%)
    all_to_all x1, waiting for transfers between devices, shards(): back = lax.all_to_all(back, both, split_axis=0, concat_axis=0)  185 us
    dot_general x8, matrix products, dot(): jnp.einsum(formula, left, right, precision=HIGH, preferred_element_type=F32)  132 us
    all_to_all x1, waiting for transfers between devices, shards(): sent = lax.all_to_all(sent, both, split_axis=1, concat_axis=0)  93.1 us
    all_to_all x1, waiting for transfers between devices, shards(): tiles = lax.all_to_all(coeffs, 'gy', split_axis=0, concat_axis=0)  92.7 us
    all_to_all x1, waiting for transfers between devices, shards(): slab = lax.all_to_all(slab, 'gy', split_axis=0, concat_axis=0)  48.9 us
    another operation x4, other arithmetic, turned(): jnp.stack([values[0] * real - values[1] * imag, values[0] * imag + values...  38 us
    sub x4, other arithmetic, turned(): values[0] * real - values[1] * imag  33.6 us
    another operation x1, local copies, waits for them, and re-layouts, turned(): jnp.stack([values[0] * real - values[1] * imag, values[0] * imag + values...  32.1 us
  transfers between devices with their start and end apart: 6, of which 5 were waited for; matrix products, arithmetic and copies ran while one was open for 18% of the time, Pallas kernels for 0%

profile of v1, /device:TPU:0, one launch (start us, length us, event | category | flops | bytes accessed | tf_op | source)
XLA Modules:
  0.0 867.2 jit_solution(10363886510317006540)
XLA Ops:
  11.7 48.9 %all-to-all-done.1 = f16[8,256,1024]{2,1,0:T(8,128)(2,1)} async-done(((f16[8,256,1024]{2,1,0:T(8,128)(2,1)}), f16[8,256,1024]{2,1,0:T(8,128)(2,1)}, u32[]{:S(2)}, u32[]{:S(2)}) %all-to-all-start.1) | async-done | bytes 4194336 | tf_op jit(solution)/shard_map/all_to_all | solution.py:114
  67.6 7.1 copy.146
  74.7 9.1 %convolution_bitcast_fusion.1 = f32[2,64,256,128]{3,1,2,0:T(8,128)S(1)} fusion(f32[8,8,2,64,1]{3,0,1,4,2:T(8,128)S(1)} %copy-done.9, f16[8,256,8,128]{3,0,2,1:T(8,128)(2,1)} %copy.146), kind=kOutput, calls=%fused_computation.39 | convolution fusion | flops 1610612736 | bytes 21004288 | tf_op jit(solution)/shard_map/hgck,hrgb->ckrb/dot_general | solution.py:38
  84.0 7.0 multiply_subtract_fusion.2
  91.0 11.9 %pad_maximum_fusion.1 = f32[2,64,256,128]{3,1,2,0:T(8,128)} fusion(f32[1,64,256,128]{3,1,2,0:T(8,128)} %get-tuple-element.20, f32[1,64,256,128]{3,1,2,0:T(8,128)} %get-tuple-element.19), kind=kLoop, calls=%fused_computation.7 | loop fusion | flops 4194304 | bytes 33554432 | tf_op jit(solution)/shard_map/stack | solution.py:43
  102.9 23.0 %fusion.27 = f32[2,64,64,256]{3,1,2,0:T(8,128)S(1)} fusion(f32[2,128,2,64,1]{1,3,0,4,2:T(8,128)S(1)} %copy-done.6, f32[2,64,256,128]{3,1,2,0:T(8,128)} %pad_maximum_fusion.1), kind=kOutput, calls=%fused_computation.55 | convolution fusion | flops 3221225472 | bytes 25296896 | tf_op jit(solution)/shard_map/cbdm,ckrb->dmkr/dot_general | solution.py:38
  142.3 93.1 %all-to-all-done.2 = f16[1,2,32,128,256]{4,3,1,0,2:T(8,128)(2,1)} async-done(((f16[1,2,32,128,256]{4,3,1,0,2:T(8,128)(2,1)}), f16[1,2,32,128,256]{4,3,1,0,2:T(8,128)(2,1)}, u32[]{:S(2)}, u32[]{:S(2)}) %all-to-all-start.2) | async-done | bytes 4194336 | tf_op jit(solution)/shard_map/all_to_all | solution.py:128
  248.6 10.4 %copy.152 = f32[32,2,128,2,128]{4,0,3,1,2:T(8,128)} copy(f32[32,2,128,2,128]{2,4,3,1,0:T(8,128)} %bitcast.244) | data formatting | bytes 16777216 | tf_op jit(solution)/shard_map/mul | solution.py:133
  269.5 10.8 %fusion.21 = f32[2,64,128,128]{3,2,0,1:T(8,128)S(1)} fusion(f32[2,128,2,128,1]{3,1,0,2,4:T(8,128)S(1)} %copy-done.2, f32[2,64,128,128,1]{3,1,2,0,4:T(8,128)S(1)} %maximum_bitcast_fusion.2), kind=kOutput, calls=%fused_computation.53 | convolution fusion | flops 3221225472 | bytes 17039360 | tf_op jit(solution)/shard_map/cbdm,cknb->dknm/dot_general | solution.py:38
  288.6 7.5 multiply_select_fusion.3
  304.2 12.6 %fusion.14 = f32[2,2,64,128,128]{4,3,0,2,1:T(8,128)} fusion(f32[2,128,2,128,1,1]{3,1,0,2,5,4:T(8,128)S(1)} %copy-done.1, f32[1,2,64,128,128]{4,3,1,2,0:T(8,128)} %maximum_bitcast_fusion.4, f32[1,2,64,128,128]{4,3,1,2,0:T(8,128)S(1)} %maximum_bitcast_fusion.3), kind=kOutput, calls=%fused_computation.38 | convolution fusion | flops 6446645248 | bytes 33816576 | tf_op jit(solution)/shard_map/cmdb,cfknm->dfknb/dot_general | solution.py:38
  316.7 7.1 multiply_subtract_fusion.1
  329.9 24.6 %bitcast_convert_fusion.1 = bf16[2,128,128,2,64]{2,4,3,1,0:T(8,128)(2,1)} fusion(f32[2,64,2,64,1,1]{1,3,0,2,5,4:T(8,128)S(1)} %copy-done.4, f32[2,2,64,128,128,1]{4,3,0,2,1,5:T(8,128)} %maximum_bitcast_fusion.1), kind=kOutput, calls=%fused_computation.11 | convolution fusion | flops 3225419776 | bytes 25231360 | tf_op jit(solution)/shard_map/ckda,cfknb->adfnb/dot_general | solution.py:38
  354.5 16.3 %copy.164 = bf16[32,2,2,2,128,128]{5,4,3,2,1,0:T(8,128)(2,1)} copy(bf16[32,2,2,2,128,128]{5,1,0,2,4,3:T(2,128)(2,1)} %bitcast.242) | data formatting | bytes 16777216 | tf_op jit(solution)/shard_map/reshape | solution.py:183
  376.0 185.0 %all-to-all-done.3 = bf16[32,2,2,2,128,128]{5,4,3,2,1,0:T(8,128)(2,1)} async-done(((bf16[32,2,2,2,128,128]{5,4,3,2,1,0:T(8,128)(2,1)}), bf16[32,2,2,2,128,128]{5,4,3,2,1,0:T(8,128)(2,1)}, u32[]{:S(2)}, u32[]{:S(2)}) %all-to-all-start.3) | async-done | bytes 8388640 | tf_op jit(solution)/shard_map/all_to_all | solution.py:187
  564.6 25.1 %convolution_bitcast_fusion = f32[2,2,2,64,128,128]{4,5,0,3,2,1:T(8,128)} fusion(f32[2,32,2,2,128,1,1,1]{4,1,2,0,3,7,6,5:T(8,128)S(1)} %copy-done.3, bf16[32,2,2,2,2,64,128,1]{6,5,4,3,2,1,0,7:T(8,128)(2,1)} %bitcast.65), kind=kOutput, calls=%fused_computation.21 | convolution fusion | flops 6442450944 | bytes 42074112 | tf_op jit(solution)/shard_map/csmdb,sgcfmky->dgfkby/dot_general | solution.py:38
  589.8 17.4 %multiply_subtract_fusion = (f32[1,2,2,64,128,128]{4,5,0,3,2,1:T(8,128)S(1)}, f32[1,2,2,64,128,128]{4,5,0,3,2,1:T(8,128)}) fusion(f32[2,2,2,64,128,128]{4,5,0,3,2,1:T(8,128)} %convolution_bitcast_fusion, f32[64,128]{1,0:T(8,128)S(1)} %get-tuple-element.70, f32[64,128]{1,0:T(8,128)S(1)} %get-tuple-element.71, ...), kind=kLoop, calls=%fused_computation.20 | loop fusion | flops 33554432 | bytes 67436608 | tf_op jit(solution)/shard_map/sub | solution.py:44
  607.1 18.4 %pad_maximum_fusion = f32[2,2,2,64,128,128]{4,5,0,3,2,1:T(8,128)} fusion(f32[1,2,2,64,128,128]{4,5,0,3,2,1:T(8,128)} %get-tuple-element.16, f32[1,2,2,64,128,128]{4,5,0,3,2,1:T(8,128)S(1)} %get-tuple-element.15), kind=kLoop, calls=%fused_computation.5 | loop fusion | flops 8388608 | bytes 67108864 | tf_op jit(solution)/shard_map/stack | solution.py:43
  625.6 32.1 %copy.166 = f32[2,2,2,64,128,128]{5,3,0,4,2,1:T(8,128)} copy(f32[2,2,2,64,128,128]{4,5,0,3,2,1:T(8,128)} %pad_maximum_fusion) | data formatting | bytes 67108864 | tf_op jit(solution)/shard_map/stack | solution.py:43
  657.7 19.6 %fusion.7 = bf16[64,2,2,128,128]{4,0,3,2,1:T(8,128)(2,1)} fusion(f32[2,2,2,64,128,128]{5,3,0,4,2,1:T(8,128)} %copy.166, f32[2,64,64,1,1,1]{1,2,0,5,4,3:T(8,128)S(1)} %copy-done.8), kind=kOutput, calls=%fused_computation.22 | convolution fusion | flops 3225419776 | bytes 41975808 | tf_op jit(solution)/shard_map/cka,cgfkby->agfby/dot_general | solution.py:38
  677.3 12.0 %copy.167 = bf16[64,2,2,128,128]{4,3,2,1,0:T(8,128)(2,1)} copy(bf16[64,2,2,128,128]{4,0,3,2,1:T(8,128)(2,1)} %fusion.7) | data formatting | bytes 16777216 | tf_op jit(solution)/shard_map/convert_element_type | solution.py:207
  695.6 92.7 %all-to-all-done.4 = bf16[8,16,2,128,128]{4,3,2,1,0:T(8,128)(2,1)} async-done(((bf16[8,16,2,128,128]{4,3,2,1,0:T(8,128)(2,1)}), bf16[8,16,2,128,128]{4,3,2,1,0:T(8,128)(2,1)}, u32[]{:S(2)}, u32[]{:S(2)}) %all-to-all-start.4) | async-done | bytes 8388640 | tf_op jit(solution)/shard_map/all_to_all | solution.py:211
  824.8 22.7 %all-to-all-done.5 = bf16[32,2,128,128]{3,2,1,0:T(8,128)(2,1)} async-done(((bf16[32,2,128,128]{3,2,1,0:T(8,128)(2,1)}), bf16[32,2,128,128]{3,2,1,0:T(8,128)(2,1)}, u32[]{:S(2)}, u32[]{:S(2)}) %all-to-all-start.5) | async-done | bytes 2097184 | tf_op jit(solution)/shard_map/all_to_all | solution.py:247
  849.8 9.5 %fusion.19 = f32[16,2,256]{2,1,0:T(2,128)S(1)} fusion(f32[16,256,128]{1,2,0:T(8,128)} %copy.172, f32[16,256]{1,0:T(8,128)S(1)} %get-tuple-element.54, s32[16,256]{1,0:T(8,128)S(1)} %get-tuple-element.48, f32[16,256]{1,0:T(8,128)S(1)} %get-tuple-element.53, s32[16,256]{1,0:T(8,128)S(1)} %get-tuple-element.47, f32[16,256]{1,0:T(8,128)S(1)} %get-tuple-element.55, ...), kind=kOutput, calls=%fused_computation.42 | convolution fusion | flops 277340160 | bytes 3309584 | tf_op jit(solution)/shard_map/scr,sdtr->sdct/dot_general | solution.py:95
  (135 shorter events, 142.1 us)
Async XLA Ops:
  6.3 54.4 %all-to-all-start.1 = ((f16[8,256,1024]{2,1,0:T(8,128)(2,1)}), f16[8,256,1024]{2,1,0:T(8,128)(2,1)}, u32[]{:S(2)}, u32[]{:S(2)}) async-start(f16[8,256,1024]{2,1,0:T(8,128)(2,1)} %bitcast.245), calls=%async_computation.1 | async-start | bytes 8388608 | tf_op jit(solution)/shard_map/all_to_all | solution.py:114
  11.5 56.1 %copy-start.12 = (pred[64]{0:T(512)(128)(4,1)}, pred[64]{0:T(512)(128)(4,1)S(1)}, u32[]{:S(2)}) copy-start(pred[64]{0:T(512)(128)(4,1)S(1)} %iota_compare_fusion.12) | copy-start | bytes 196
  67.6 7.1 copy-start.9
  91.0 11.9 %copy-start.6 = (f32[2,128,2,64,1]{1,3,0,4,2:T(8,128)S(1)}, f32[2,128,2,64,1]{1,3,0,4,2:T(8,128)}, u32[]{:S(2)}) copy-start(f32[2,128,2,64,1]{1,3,0,4,2:T(8,128)} %constant.299) | copy-start | bytes 393220
  102.9 23.0 %copy-start.14 = (f32[128]{0:T(128)S(1)}, f32[128]{0:T(128)}, u32[]{:S(2)}) copy-start(f32[128]{0:T(128)} %constant.287.clone) | copy-start | bytes 1540
  136.8 98.6 %all-to-all-start.2 = ((f16[1,2,32,128,256]{4,3,1,0,2:T(8,128)(2,1)}), f16[1,2,32,128,256]{4,3,1,0,2:T(8,128)(2,1)}, u32[]{:S(2)}, u32[]{:S(2)}) async-start(f16[1,2,32,128,256]{4,3,1,0,2:T(8,128)(2,1)} %copy.150), calls=%async_computation.2 | async-start | bytes 8388608 | tf_op jit(solution)/shard_map/all_to_all | solution.py:128
  248.6 10.4 %copy-start.5 = (f32[2,32,2,2,64,1]{4,1,2,0,5,3:T(8,128)S(1)}, f32[2,32,2,2,64,1]{4,1,2,0,5,3:T(8,128)}, u32[]{:S(2)}) copy-start(f32[2,32,2,2,64,1]{4,1,2,0,5,3:T(8,128)} %constant.298) | copy-start | bytes 196612
  267.9 1.7 copy-start.2
  280.3 3.2 copy-start
  300.1 4.1 copy-start.1
  323.9 6.1 copy-start.4
  370.9 4.3 copy-start.15
  370.9 193.7 %copy-start.3 = (f32[2,32,2,2,128,1,1,1]{4,1,2,0,3,7,6,5:T(8,128)S(1)}, f32[2,32,2,2,128,1,1,1]{4,1,2,0,3,7,6,5:T(8,128)}, u32[]{:S(2)}) copy-start(f32[2,32,2,2,128,1,1,1]{4,1,2,0,3,7,6,5:T(8,128)} %constant.304) | copy-start | bytes 393220
  370.9 190.2 %all-to-all-start.3 = ((bf16[32,2,2,2,128,128]{5,4,3,2,1,0:T(8,128)(2,1)}), bf16[32,2,2,2,128,128]{5,4,3,2,1,0:T(8,128)(2,1)}, u32[]{:S(2)}, u32[]{:S(2)}) async-start(bf16[32,2,2,2,128,128]{5,4,3,2,1,0:T(8,128)(2,1)} %copy.164), calls=%async_computation.3 | async-start | bytes 16777216 | tf_op jit(solution)/shard_map/all_to_all | solution.py:187
  561.0 128.3 %all-to-all-start = ((s32[32,1,1]{2,1,0:T(1,128)}), s32[32,1,1]{2,1,0:T(1,128)S(1)}, u32[]{:S(2)}, u32[]{:S(2)}) async-start(s32[32,1,1]{2,1,0:T(1,128)} %copy.144), calls=%async_computation | async-start | bytes 32768 | tf_op jit(solution)/shard_map/all_to_all | solution.py:245
  564.6 25.2 %copy-start.13 = (pred[64]{0:T(512)(128)(4,1)S(1)}, pred[64]{0:T(512)(128)(4,1)}, u32[]{:S(2)}) copy-start(pred[64]{0:T(512)(128)(4,1)} %copy-done.12) | copy-start | bytes 196
  625.5 32.1 %copy-start.8 = (f32[2,64,64,1,1,1]{1,2,0,5,4,3:T(8,128)S(1)}, f32[2,64,64,1,1,1]{1,2,0,5,4,3:T(8,128)}, u32[]{:S(2)}) copy-start(f32[2,64,64,1,1,1]{1,2,0,5,4,3:T(8,128)} %constant.305) | copy-start | bytes 98308
  689.3 99.0 %all-to-all-start.4 = ((bf16[8,16,2,128,128]{4,3,2,1,0:T(8,128)(2,1)}), bf16[8,16,2,128,128]{4,3,2,1,0:T(8,128)(2,1)}, u32[]{:S(2)}, u32[]{:S(2)}) async-start(bf16[8,16,2,128,128]{4,3,2,1,0:T(8,128)(2,1)} %bitcast.243), calls=%async_computation.4 | async-start | bytes 16777216 | tf_op jit(solution)/shard_map/all_to_all | solution.py:211
  792.6 6.1 copy-start.7
  792.7 11.3 %copy-start.10 = (f32[2,2048]{1,0:T(2,128)S(1)}, f32[2,2048]{1,0:T(2,128)}, u32[]{:S(2)}) copy-start(f32[2,2048]{1,0:T(2,128)} %param.19) | copy-start | bytes 49156
  794.2 53.2 %all-to-all-start.5 = ((bf16[32,2,128,128]{3,2,1,0:T(8,128)(2,1)}), bf16[32,2,128,128]{3,2,1,0:T(8,128)(2,1)}, u32[]{:S(2)}, u32[]{:S(2)}) async-start(bf16[32,2,128,128]{3,2,1,0:T(8,128)(2,1)} %broadcast_select_fusion), calls=%async_computation.5 | async-start | bytes 4194304 | tf_op jit(solution)/shard_map/all_to_all | solution.py:247
  798.8 12.5 %copy-start.11 = (s32[2,2048]{1,0:T(2,128)S(1)}, s32[2,2048]{1,0:T(2,128)}, u32[]{:S(2)}) copy-start(s32[2,2048]{1,0:T(2,128)} %param.18) | copy-start | bytes 49156

commit v2 on v1

--- a/solution.py
+++ b/solution.py
@@ -110,31 +110,48 @@
     half_low = low // 2
     alternating = jnp.asarray(1.0 - 2.0 * (np.arange(low) % 2), F32)
 
-    slab = vorticity.astype(F16).reshape(group_cols, rows, block_cols)
-    slab = lax.all_to_all(slab, "gy", split_axis=0, concat_axis=0)
-    slab = slab.reshape(group_cols, rows, block_cols // low, low)
+    chunks = rows // low if rows % low == 0 else 1
+    piece = rows // chunks
     real, imag = root(high, high, high, -1.0)
-    table = np.stack([real, imag], 1).reshape(group_cols, block_cols // low, 2, high)
-    first = dot("hgck,hrgb->ckrb", table.astype(np.float32), slab.astype(F32))
+    row_table = np.stack([real, imag], 1).reshape(group_cols, block_cols // low, 2, high)
+    row_table = row_table.astype(np.float32)
     twist = twiddle_table(high, low, length, -1.0)
-    nyquist = jnp.sum(first[0, 0] * alternating[None, :], axis=-1)
-    first = turned(first, twist, (high, 1, low))
-    spec = dot("cbdm,ckrb->dmkr", mixing(low, half_low, low, -1.0), first)
     here = jnp.logical_and(
         jnp.arange(half_low)[:, None] == 0, jnp.arange(high)[None, :] == 0
     )[:, :, None]
-    spec = jnp.stack([spec[0], jnp.where(here, nyquist[None, None, :], spec[1])])
-    sent = (spec * 0.125).reshape(2, devices, cols, rows).astype(F16)
-    sent = lax.all_to_all(sent, both, split_axis=1, concat_axis=0)
-
-    if rows % low == 0:
-        got = sent.reshape(devices, 2, cols, rows // low, low)
-        table = mixing(high, high, high, -1.0).reshape(2, devices, rows // low, 2, high)
-        second = dot("csgdk,scngb->dknb", table, got.astype(F32) * 8.0)
-    else:
-        got = sent.reshape(high, low // rows, 2, cols, rows).transpose(0, 2, 3, 1, 4)
-        got = got.reshape(high, 2, cols, low)
-        second = dot("cadk,acnb->dknb", mixing(high, high, high, -1.0), got.astype(F32) * 8.0)
+    blocks = vorticity.reshape(group_cols, chunks, piece, block_cols)
+    slabs = [
+        lax.all_to_all(blocks[:, chunk].astype(F16), "gy", split_axis=0, concat_axis=0)
+        for chunk in range(chunks)
+    ]
+    if chunks > 1:
+        col_table = mixing(high, high, high, -1.0).reshape(2, devices, chunks, 2, high)
+    second = None
+    for chunk in range(chunks):
+        slab = slabs[chunk]
+        slab = slab.reshape(group_cols, piece, block_cols // low, low)
+        first = dot("hgck,hrgb->ckrb", row_table, slab.astype(F32))
+        nyquist = jnp.sum(first[0, 0] * alternating[None, :], axis=-1)
+        first = turned(first, twist, (high, 1, low))
+        spec = dot("cbdm,ckrb->dmkr", mixing(low, half_low, low, -1.0), first)
+        spec = jnp.stack([spec[0], jnp.where(here, nyquist[None, None, :], spec[1])])
+        sent = (spec * 0.125).reshape(2, devices, cols, piece).astype(F16)
+        if chunk + 1 < chunks:
+            sent, slabs[chunk + 1] = lax.optimization_barrier((sent, slabs[chunk + 1]))
+        sent = lax.all_to_all(sent, both, split_axis=1, concat_axis=0)
+        if rows % low == 0:
+            got = sent.reshape(devices, 2, cols, low).astype(F32) * 8.0
+            table = (
+                mixing(high, high, high, -1.0).reshape(2, devices, 2, high)
+                if chunks == 1
+                else col_table[:, :, chunk]
+            )
+            part = dot("csdk,scnb->dknb", table, got)
+        else:
+            got = sent.reshape(high, low // rows, 2, cols, rows).transpose(0, 2, 3, 1, 4)
+            got = got.reshape(high, 2, cols, low).astype(F32) * 8.0
+            part = dot("cadk,acnb->dknb", mixing(high, high, high, -1.0), got)
+        second = part if second is None else second + part
     second = turned(second, twist, (high, 1, low))
     full = dot("cbdm,cknb->dknm", mixing(low, low, low, -1.0), second)
 
@@ -167,57 +184,59 @@
     def place(edge, values):
         return jnp.where(on_edge, edge.reshape(low, high).T[:, None, :], values)
 
-    fields = jnp.stack(
-        [
-            jnp.stack([place(eu_real[0] - eu_imag[1], u_real), place(ev_real[0] - ev_imag[1], v_real)]),
-            jnp.stack([place(eu_imag[0] + eu_real[1], u_imag), place(ev_imag[0] + ev_real[1], v_imag)]),
-        ]
-    )
-
-    third = dot("cmdb,cfknm->dfknb", mixing(low, low, low, 1.0), fields)
+    fields = (
+        jnp.stack([place(eu_real[0] - eu_imag[1], u_real), place(eu_imag[0] + eu_real[1], u_imag)]),
+        jnp.stack([place(ev_real[0] - ev_imag[1], v_real), place(ev_imag[0] + ev_real[1], v_imag)]),
+    )
     untwist = twiddle_table(high, low, length, 1.0)
-    third = turned(third, untwist, (1, high, 1, low))
-    back = dot("ckda,cfknb->adfnb", mixing(high, high, high, 1.0), third)
-    back = back.astype(BF16)
-    if rows % low == 0:
-        back = back.reshape(devices, rows // low, 2, 2, cols, low)
-    else:
-        back = back.reshape(high, 2, 2, cols, low // rows, rows).transpose(0, 4, 1, 2, 3, 5)
-        back = back.reshape(devices, 1, 2, 2, cols, rows)
-    back = lax.all_to_all(back, both, split_axis=0, concat_axis=0)
-
-    groups, lanes = back.shape[1], back.shape[-1]
-    if cols % high == 0:
-        back = back.reshape(devices * groups, 2, 2, cols // high, high, lanes)
-        back = back.reshape(devices, groups, 2, 2, cols // high, high, lanes)
-        table = mixing(half_low, low, low, 1.0).reshape(2, devices, cols // high, 2, low)
-        fourth = dot("csmdb,sgcfmky->dgfkby", table, back.astype(F32))
-        nyquist = back[0, :, 1, :, 0, 0]
-    else:
-        back = back.reshape(half_low, high // cols, groups, 2, 2, cols, lanes)
-        back = back.transpose(0, 2, 3, 4, 1, 5, 6).reshape(half_low, groups, 2, 2, high, lanes)
-        fourth = dot("cmdb,mgcfky->dgfkby", mixing(half_low, low, low, 1.0), back.astype(F32))
-        nyquist = back[0, :, 1, :, 0]
-    lift = nyquist.astype(F32)[:, :, None, None, :] * alternating[None, None, None, :, None]
-    first_k = (jnp.arange(high) == 0)[None, None, :, None, None]
-    fourth = jnp.stack([fourth[0] + jnp.where(first_k, lift, 0.0), fourth[1]])
-    fourth = turned(fourth, untwist, (1, 1, high, low, 1))
     real, imag = root(high, high, high, 1.0)
-    table = np.stack([real, -imag]).astype(np.float32) / (length * length)
-    coeffs = dot("cka,cgfkby->agfby", table, fourth).astype(BF16)
+    end_table = np.stack([real, -imag]).astype(np.float32) / (length * length)
+    first_k = (jnp.arange(high) == 0)[None, :, None, None]
     tile_rows = block_rows // TILE
     tile_cols = block_cols // TILE
-    coeffs = coeffs.reshape(group_cols, tile_cols * groups, 2, TILE, lanes)
-    tiles = lax.all_to_all(coeffs, "gy", split_axis=0, concat_axis=0)
-    if lanes == TILE:
-        tiles = tiles.reshape(group_cols, tile_cols, groups, 2, TILE, TILE)
-        tile_groups = groups
-    else:
-        parts = TILE // lanes
-        tiles = tiles.reshape(group_cols // parts, parts, tile_cols, 2, TILE, lanes)
-        tiles = tiles.transpose(0, 2, 3, 4, 1, 5)
-        tile_groups = 1
-    tiles = tiles.reshape(tile_rows * tile_cols, 2, TILE, TILE)
+
+    def columns_back(field):
+        third = dot("cmdb,cknm->dknb", mixing(low, low, low, 1.0), field)
+        third = turned(third, untwist, (high, 1, low))
+        back = dot("ckda,cknb->adnb", mixing(high, high, high, 1.0), third).astype(BF16)
+        if rows % low == 0:
+            back = back.reshape(devices, rows // low, 2, cols, low)
+        else:
+            back = back.reshape(high, 2, cols, low // rows, rows).transpose(0, 3, 1, 2, 4)
+            back = back.reshape(devices, 1, 2, cols, rows)
+        return lax.all_to_all(back, both, split_axis=0, concat_axis=0)
+
+    def rows_back(back, later):
+        groups, lanes = back.shape[1], back.shape[-1]
+        if cols % high == 0:
+            back = back.reshape(devices, groups, 2, cols // high, high, lanes)
+            table = mixing(half_low, low, low, 1.0).reshape(2, devices, cols // high, 2, low)
+            fourth = dot("csmdb,sgcmky->dgkby", table, back.astype(F32))
+            nyquist = back[0, :, 1, 0, 0]
+        else:
+            back = back.reshape(half_low, high // cols, groups, 2, cols, lanes)
+            back = back.transpose(0, 2, 3, 1, 4, 5).reshape(half_low, groups, 2, high, lanes)
+            fourth = dot("cmdb,mgcky->dgkby", mixing(half_low, low, low, 1.0), back.astype(F32))
+            nyquist = back[0, :, 1, 0]
+        lift = nyquist.astype(F32)[:, None, None, :] * alternating[None, None, :, None]
+        fourth = jnp.stack([fourth[0] + jnp.where(first_k, lift, 0.0), fourth[1]])
+        fourth = turned(fourth, untwist, (1, high, low, 1))
+        coeffs = dot("cka,cgkby->agby", end_table, fourth).astype(BF16)
+        coeffs = coeffs.reshape(group_cols, tile_cols * groups, TILE, lanes)
+        if later is not None:
+            coeffs, later = lax.optimization_barrier((coeffs, later))
+        tiles = lax.all_to_all(coeffs, "gy", split_axis=0, concat_axis=0)
+        if lanes != TILE:
+            parts = TILE // lanes
+            tiles = tiles.reshape(group_cols // parts, parts, tile_cols, TILE, lanes)
+            tiles = tiles.transpose(0, 2, 3, 1, 4)
+        return tiles.reshape(tile_rows * tile_cols, TILE, TILE), later
+
+    received = [columns_back(field) for field in fields]
+    u_tiles, waiting = rows_back(received[0], received[1])
+    v_tiles, _ = rows_back(waiting, None)
+    tiles = [u_tiles, v_tiles]
+    tile_groups = rows // TILE if rows % TILE == 0 else 1
 
     wanted = tile_list[0]
     tile_count = wanted.shape[0]
@@ -243,7 +262,8 @@
     owns = (owner_index[:, None] == jnp.arange(devices, dtype=jnp.int32)[None, :]).astype(jnp.int32)
     request = jnp.sum(owns * (local_index[:, None] + 1), axis=0) - 1
     request = lax.all_to_all(request, both, split_axis=0, concat_axis=0, tiled=True)
-    outgoing = jnp.take(tiles, jnp.maximum(request, 0), axis=0)
+    asked = jnp.maximum(request, 0)
+    outgoing = jnp.stack([jnp.take(part, asked, axis=0) for part in tiles], axis=1)
     incoming = lax.all_to_all(outgoing, both, split_axis=0, concat_axis=0, tiled=True)
     grouped = slot_velocity(jnp.take(incoming, owner_index, axis=0), grouped_cell, grouped_frac)
     flattened = grouped.transpose(1, 0, 2).reshape(2, tile_count * capacity)

time: 875 us -> 742 us (0.85)
  waiting for transfers between devices: 442 us -> 282 us
  blocking collectives: 0 us -> 53.5 us
  other arithmetic: 119 us -> 93.5 us
  starting transfers between devices: 26.5 us -> 41.7 us
  matrix products: 141 us -> 131 us
  local copies, waits for them, and re-layouts: 137 us -> 128 us
    all_to_all x3 -> x5, waiting for transfers between devices: 327 us -> 175 us  [the longest x2 104 us: columns_back(): return lax.all_to_all(back, both, split_axis=0, concat_axis=0)]
    all_to_all x0 -> x1, blocking collectives: none -> 53.5 us  [rows_back(): tiles = lax.all_to_all(coeffs, 'gy', split_axis=0, concat_axis=0)]
    all_to_all x2 -> x1, local copies, waits for them, and re-layouts: 13.7 us -> 2.81 us  [shards(): lax.all_to_all(blocks[:, chunk].astype(F16), 'gy', split_axis=0, concat_a...]
    dot_general x8 -> x15, matrix products: 132 us -> 121 us  [dot(): jnp.einsum(formula, left, right, precision=HIGH, preferred_element_type=F32)]
    mul x1 -> x0, local copies, waits for them, and re-layouts: 10.4 us -> none  [shards(): second = dot('csgdk,scngb->dknb', table, got.astype(F32) * 8.0)]
    all_to_all x1 -> x2, waiting for transfers between devices: 93.1 us -> 84.5 us  [shards(): sent = lax.all_to_all(sent, both, split_axis=1, concat_axis=0)]
    all_to_all x3 -> x5, starting transfers between devices: 14.4 us -> 23 us  [the longest x2 9.55 us: shards(): lax.all_to_all(blocks[:, chunk].astype(F16), 'gy', split_axis=0, concat_a...]
    sub x4 -> x6, other arithmetic: 33.6 us -> 26.7 us  [turned(): values[0] * real - values[1] * imag]
  transfers between devices with their start and end apart: 6 -> 9, of which waited for: 5 -> 7; matrix products, arithmetic and copies ran while one was open for 18% -> 29% of each run, Pallas kernels for 0% -> 0%
where the time goes in v2:
time: 742 us; the launch traced here: 730 us
  waiting for transfers between devices  282 us (38%)
  matrix products  131 us (18%)
  local copies, waits for them, and re-layouts  128 us (17%)
  other arithmetic  93.5 us (13%)
  blocking collectives  53.5 us (7%)
  starting transfers between devices  41.7 us (6%)
    dot_general x15, matrix products, dot(): jnp.einsum(formula, left, right, precision=HIGH, preferred_element_type=F32)  121 us
    all_to_all x2, waiting for transfers between devices, columns_back(): return lax.all_to_all(back, both, split_axis=0, concat_axis=0)  104 us
    all_to_all x2, waiting for transfers between devices, shards(): sent = lax.all_to_all(sent, both, split_axis=1, concat_axis=0)  84.5 us
    all_to_all x1, blocking collectives, rows_back(): tiles = lax.all_to_all(coeffs, 'gy', split_axis=0, concat_axis=0)  53.5 us
    all_to_all x1, waiting for transfers between devices, rows_back(): tiles = lax.all_to_all(coeffs, 'gy', split_axis=0, concat_axis=0)  45.5 us
    another operation x7, other arithmetic, turned(): jnp.stack([values[0] * real - values[1] * imag, values[0] * imag + values...  35.5 us
    another operation x2, local copies, waits for them, and re-layouts, turned(): jnp.stack([values[0] * real - values[1] * imag, values[0] * imag + values...  33 us
    sub x6, other arithmetic, turned(): values[0] * real - values[1] * imag  26.7 us
  transfers between devices with their start and end apart: 9, of which 7 were waited for; matrix products, arithmetic and copies ran while one was open for 29% of the time, Pallas kernels for 0%

profile of v2, /device:TPU:0, one launch (start us, length us, event | category | flops | bytes accessed | tf_op | source)
XLA Modules:
  0.0 730.3 jit_solution(13297255898524615056)
XLA Ops:
  13.0 26.4 %all-to-all-done = f16[8,128,1024]{2,1,0:T(8,128)(2,1)S(1)} async-done(((f16[8,128,1024]{2,1,0:T(8,128)(2,1)}), f16[8,128,1024]{2,1,0:T(8,128)(2,1)S(1)}, u32[]{:S(2)}, u32[]{:S(2)}) %all-to-all-start) | async-done | bytes 2097184 | tf_op jit(solution)/shard_map/all_to_all | solution.py:124
  58.2 8.8 %fusion.45 = f32[2,64,64,128]{3,1,2,0:T(8,128)S(1)} fusion(f32[2,128,2,64,1]{1,3,0,4,2:T(8,128)S(1)} %copy-done.4, f32[2,64,128,128]{3,1,2,0:T(8,128)S(1)} %pad_maximum_fusion.2), kind=kOutput, calls=%fused_computation.87 | convolution fusion | flops 1610612736 | bytes 12713984 | tf_op jit(solution)/shard_map/cbdm,ckrb->dmkr/dot_general | solution.py:38
  87.7 8.6 %fusion.48 = f32[2,64,64,128]{3,1,2,0:T(8,128)S(1)} fusion(f32[2,128,2,64,1]{1,3,0,4,2:T(8,128)S(1)} %copy-done.4, f32[2,64,128,128]{3,1,2,0:T(8,128)S(1)} %pad_maximum_fusion.3), kind=kOutput, calls=%fused_computation.88 | convolution fusion | flops 1610612736 | bytes 12713984 | tf_op jit(solution)/shard_map/cbdm,ckrb->dmkr/dot_general | solution.py:38
  116.8 42.7 %all-to-all-done.3 = f16[1,2,32,128,128]{4,1,3,0,2:T(2,128)(2,1)S(1)} async-done(((f16[1,2,32,128,128]{4,1,3,0,2:T(2,128)(2,1)}), f16[1,2,32,128,128]{4,1,3,0,2:T(2,128)(2,1)S(1)}, u32[]{:S(2)}, u32[]{:S(2)}) %all-to-all-start.3) | async-done | bytes 2097184 | tf_op jit(solution)/shard_map/all_to_all | solution.py:141
  170.7 41.7 %all-to-all-done.2 = f16[1,2,32,128,128]{4,1,3,0,2:T(2,128)(2,1)} async-done(((f16[1,2,32,128,128]{4,1,3,0,2:T(2,128)(2,1)}), f16[1,2,32,128,128]{4,1,3,0,2:T(2,128)(2,1)}, u32[]{:S(2)}, u32[]{:S(2)}) %all-to-all-start.2) | async-done | bytes 2097184 | tf_op jit(solution)/shard_map/all_to_all | solution.py:141
  212.5 10.0 %fusion.12 = f32[2,64,128,128]{3,1,2,0:T(8,128)S(1)} fusion(f32[128,128,2,64,1]{1,3,4,0,2:T(8,128)} %fusion.23, f32[2,32,2,64,1]{3,1,0,4,2:T(8,128)S(1)} %copy-done.9, f16[1,2,32,128,128]{4,1,3,0,2:T(2,128)(2,1)} %all-to-all-done.2), kind=kOutput, calls=%fused_computation.34 | convolution fusion | flops 809500672 | bytes 18907136 | tf_op jit(solution)/shard_map/csdk,scnb->dknb/dot_general | solution.py:38
  226.2 10.8 %fusion.34 = f32[2,64,128,128]{3,2,0,1:T(8,128)S(1)} fusion(f32[2,128,2,128,1]{3,1,0,2,4:T(8,128)S(1)} %copy-done.5, f32[2,64,128,128,1]{3,1,2,0,4:T(8,128)S(1)} %maximum_bitcast_fusion), kind=kOutput, calls=%fused_computation.82 | convolution fusion | flops 3221225472 | bytes 17039360 | tf_op jit(solution)/shard_map/cbdm,cknb->dknm/dot_general | solution.py:38
  267.0 11.7 %bitcast_convert_fusion.3 = bf16[128,128,2,64]{1,3,2,0:T(8,128)(2,1)S(1)} fusion(f32[2,64,2,64,1]{1,3,0,2,4:T(8,128)S(1)} %copy-done.3, f32[2,64,128,128,1]{3,2,0,1,4:T(8,128)S(1)} %maximum_bitcast_fusion.3), kind=kOutput, calls=%fused_computation.28 | convolution fusion | flops 1612709888 | bytes 12648448 | tf_op jit(solution)/shard_map/ckda,cknb->adnb/dot_general | solution.py:38
  294.0 11.7 %bitcast_convert_fusion.1 = bf16[128,128,2,64]{1,3,2,0:T(8,128)(2,1)S(1)} fusion(f32[2,64,2,64,1]{1,3,0,2,4:T(8,128)S(1)} %copy-done.3, f32[2,64,128,128,1]{3,2,0,1,4:T(8,128)S(1)} %maximum_bitcast_fusion.6), kind=kOutput, calls=%fused_computation.24 | convolution fusion | flops 1612709888 | bytes 12648448 | tf_op jit(solution)/shard_map/ckda,cknb->adnb/dot_general | solution.py:38
  312.5 71.1 %all-to-all-done.4 = bf16[32,2,2,128,128]{4,3,2,1,0:T(8,128)(2,1)} async-done(((bf16[32,2,2,128,128]{4,3,2,1,0:T(8,128)(2,1)}), bf16[32,2,2,128,128]{4,3,2,1,0:T(8,128)(2,1)}, u32[]{:S(2)}, u32[]{:S(2)}) %all-to-all-start.4) | async-done | bytes 4194336 | tf_op jit(solution)/shard_map/all_to_all | solution.py:207
  389.7 10.2 %convolution_bitcast_fusion.1 = f32[2,2,64,128,128]{3,4,0,2,1:T(8,128)S(1)} fusion(f32[2,32,2,2,128,1,1]{4,1,2,0,3,6,5:T(8,128)S(1)} %copy-done.2, bf16[32,2,2,2,64,128,1]{5,4,3,2,1,0,6:T(8,128)(2,1)} %bitcast.81), kind=kOutput, calls=%fused_computation.46 | convolution fusion | flops 3221225472 | bytes 21102592 | tf_op jit(solution)/shard_map/csmdb,sgcmky->dgkby/dot_general | solution.py:38
  400.0 7.2 multiply_subtract_fusion.1
  407.2 11.7 %pad_maximum_fusion = f32[2,2,64,128,128]{3,4,0,2,1:T(8,128)} fusion(f32[1,2,64,128,128]{3,4,0,2,1:T(8,128)} %get-tuple-element.27, f32[1,2,64,128,128]{3,4,0,2,1:T(8,128)} %get-tuple-element.26), kind=kLoop, calls=%fused_computation.6 | loop fusion | flops 4194304 | bytes 33554432 | tf_op jit(solution)/shard_map/stack | solution.py:43
  418.9 16.5 %copy.237 = f32[2,2,64,128,128]{4,2,0,3,1:T(8,128)} copy(f32[2,2,64,128,128]{3,4,0,2,1:T(8,128)} %pad_maximum_fusion) | data formatting | bytes 33554432 | tf_op jit(solution)/shard_map/stack | solution.py:43
  435.5 9.1 %fusion.19 = bf16[64,2,128,128]{3,0,2,1:T(8,128)(2,1)S(1)} fusion(f32[2,2,64,128,128]{4,2,0,3,1:T(8,128)} %copy.237, f32[2,64,64,1,1]{1,2,0,4,3:T(8,128)S(1)} %copy-done.6), kind=kOutput, calls=%fused_computation.47 | convolution fusion | flops 1612709888 | bytes 21004288 | tf_op jit(solution)/shard_map/cka,cgkby->agby/dot_general | solution.py:38
  449.3 32.4 %all-to-all-done.5 = bf16[32,2,2,128,128]{4,3,2,1,0:T(8,128)(2,1)} async-done(((bf16[32,2,2,128,128]{4,3,2,1,0:T(8,128)(2,1)}), bf16[32,2,2,128,128]{4,3,2,1,0:T(8,128)(2,1)}, u32[]{:S(2)}, u32[]{:S(2)}) %all-to-all-start.5) | async-done | bytes 4194336 | tf_op jit(solution)/shard_map/all_to_all | solution.py:207
  485.9 10.2 %convolution_bitcast_fusion = f32[2,2,64,128,128]{3,4,0,2,1:T(8,128)S(1)} fusion(f32[2,32,2,2,128,1,1]{4,1,2,0,3,6,5:T(8,128)S(1)} %copy-done.2, bf16[32,2,2,2,64,128,1]{5,4,3,2,1,0,6:T(8,128)(2,1)} %bitcast.112), kind=kOutput, calls=%fused_computation.45 | convolution fusion | flops 3221225472 | bytes 21102592 | tf_op jit(solution)/shard_map/csmdb,sgcmky->dgkby/dot_general | solution.py:38
  504.1 11.7 %pad_maximum_fusion.1 = f32[2,2,64,128,128]{3,4,0,2,1:T(8,128)} fusion(f32[1,2,64,128,128]{3,4,0,2,1:T(8,128)} %get-tuple-element.25, f32[1,2,64,128,128]{3,4,0,2,1:T(8,128)} %get-tuple-element.24), kind=kLoop, calls=%fused_computation.7 | loop fusion | flops 4194304 | bytes 33554432 | tf_op jit(solution)/shard_map/stack | solution.py:43
  515.9 16.5 %copy.244 = f32[2,2,64,128,128]{4,2,0,3,1:T(8,128)} copy(f32[2,2,64,128,128]{3,4,0,2,1:T(8,128)} %pad_maximum_fusion.1) | data formatting | bytes 33554432 | tf_op jit(solution)/shard_map/stack | solution.py:43
  532.4 8.9 %fusion.20 = bf16[64,2,128,128]{3,0,2,1:T(8,128)(2,1)S(1)} fusion(f32[2,2,64,128,128]{4,2,0,3,1:T(8,128)} %copy.244, f32[2,64,64,1,1]{1,2,0,4,3:T(8,128)S(1)} %copy-done.6), kind=kOutput, calls=%fused_computation.48 | convolution fusion | flops 1612709888 | bytes 21004288 | tf_op jit(solution)/shard_map/cka,cgkby->agby/dot_general | solution.py:38
  545.9 53.5 %all_to_all.59 = bf16[8,16,128,128]{3,2,1,0:T(8,128)(2,1)} all-to-all(bf16[8,16,128,128]{3,2,1,0:T(8,128)(2,1)} %bitcast.334), channel_id=1, replica_groups=mesh['gx'=4,'gy'=8] {'gy'}, dimensions={0} | all-to-all | bytes 8388608 | tf_op jit(solution)/shard_map/all_to_all | solution.py:228
  607.6 45.5 %all-to-all-done.6 = bf16[8,16,128,128]{3,2,1,0:T(8,128)(2,1)} async-done(((bf16[8,16,128,128]{3,2,1,0:T(8,128)(2,1)}), bf16[8,16,128,128]{3,2,1,0:T(8,128)(2,1)}, u32[]{:S(2)}, u32[]{:S(2)}) %all-to-all-start.6) | async-done | bytes 4194336 | tf_op jit(solution)/shard_map/all_to_all | solution.py:228
  688.3 22.4 %all-to-all-done.9 = bf16[32,2,128,128]{3,2,1,0:T(8,128)(2,1)} async-done(((bf16[32,2,128,128]{3,2,1,0:T(8,128)(2,1)}), bf16[32,2,128,128]{3,2,1,0:T(8,128)(2,1)}, u32[]{:S(2)}, u32[]{:S(2)}) %all-to-all-start.9) | async-done | bytes 2097184 | tf_op jit(solution)/shard_map/all_to_all | solution.py:267
  713.1 9.5 %fusion.27 = f32[16,2,256]{2,1,0:T(2,128)S(1)} fusion(f32[16,256,128]{1,2,0:T(8,128)} %copy.250, f32[16,256]{1,0:T(8,128)S(1)} %get-tuple-element.75, s32[16,256]{1,0:T(8,128)S(1)} %get-tuple-element.69, f32[16,256]{1,0:T(8,128)S(1)} %get-tuple-element.74, s32[16,256]{1,0:T(8,128)S(1)} %get-tuple-element.68, f32[16,256]{1,0:T(8,128)S(1)} %get-tuple-element.76, ...), kind=kOutput, calls=%fused_computation.58 | convolution fusion | flops 277340160 | bytes 3309584 | tf_op jit(solution)/shard_map/scr,sdtr->sdct/dot_general | solution.py:95
  (165 shorter events, 220.2 us)
Async XLA Ops:
  7.6 31.8 %all-to-all-start = ((f16[8,128,1024]{2,1,0:T(8,128)(2,1)}), f16[8,128,1024]{2,1,0:T(8,128)(2,1)S(1)}, u32[]{:S(2)}, u32[]{:S(2)}) async-start(f16[8,128,1024]{2,1,0:T(8,128)(2,1)} %get-tuple-element.49), calls=%async_computation | async-start | bytes 4194304 | tf_op jit(solution)/shard_map/all_to_all | solution.py:124
  39.4 32.8 %all-to-all-start.1 = ((f16[8,128,1024]{2,1,0:T(8,128)(2,1)}), f16[8,128,1024]{2,1,0:T(8,128)(2,1)}, u32[]{:S(2)}, u32[]{:S(2)}) async-start(f16[8,128,1024]{2,1,0:T(8,128)(2,1)} %get-tuple-element.48), calls=%async_computation.1 | async-start | bytes 4194304 | tf_op jit(solution)/shard_map/all_to_all | solution.py:124
  43.8 6.7 copy-start.7
  50.5 3.9 copy-start.13
  56.5 1.7 copy-start.4
  104.6 54.9 %all-to-all-start.3 = ((f16[1,2,32,128,128]{4,1,3,0,2:T(2,128)(2,1)}), f16[1,2,32,128,128]{4,1,3,0,2:T(2,128)(2,1)S(1)}, u32[]{:S(2)}, u32[]{:S(2)}) async-start(f16[1,2,32,128,128]{4,1,3,0,2:T(2,128)(2,1)} %copy.223), calls=%async_computation.3 | async-start | bytes 4194304 | tf_op jit(solution)/shard_map/all_to_all | solution.py:141
  110.8 53.6 %copy-start.10 = (f32[2,32,2,64,1]{3,1,0,4,2:T(8,128)S(1)}, f32[2,32,2,64,1]{3,1,0,4,2:T(8,128)}, u32[]{:S(2)}) copy-start(f32[2,32,2,64,1]{3,1,0,4,2:T(8,128)} %constant.297) | copy-start | bytes 98308
  159.5 52.9 %all-to-all-start.2 = ((f16[1,2,32,128,128]{4,1,3,0,2:T(2,128)(2,1)}), f16[1,2,32,128,128]{4,1,3,0,2:T(2,128)(2,1)}, u32[]{:S(2)}, u32[]{:S(2)}) async-start(f16[1,2,32,128,128]{4,1,3,0,2:T(2,128)(2,1)} %copy.215), calls=%async_computation.2 | async-start | bytes 4194304 | tf_op jit(solution)/shard_map/all_to_all | solution.py:141
  164.4 48.1 %copy-start.9 = (f32[2,32,2,64,1]{3,1,0,4,2:T(8,128)S(1)}, f32[2,32,2,64,1]{3,1,0,4,2:T(8,128)}, u32[]{:S(2)}) copy-start(f32[2,32,2,64,1]{3,1,0,4,2:T(8,128)} %constant.296) | copy-start | bytes 98308
  224.5 1.7 copy-start.5
  237.0 3.2 copy-start
  245.1 5.5 copy-start.1
  264.0 3.1 copy-start.3
  285.5 98.1 %all-to-all-start.4 = ((bf16[32,2,2,128,128]{4,3,2,1,0:T(8,128)(2,1)}), bf16[32,2,2,128,128]{4,3,2,1,0:T(8,128)(2,1)}, u32[]{:S(2)}, u32[]{:S(2)}) async-start(bf16[32,2,2,128,128]{4,3,2,1,0:T(8,128)(2,1)} %copy.235), calls=%async_computation.4 | async-start | bytes 8388608 | tf_op jit(solution)/shard_map/all_to_all | solution.py:207
  312.5 75.6 %copy-start.14 = (s32[1,16]{1,0:T(1,128)S(1)}, s32[1,16]{1,0:T(1,128)}, u32[]{:S(2)}) copy-start(s32[1,16]{1,0:T(1,128)} %param.25) | copy-start | bytes 196
  312.5 77.2 %copy-start.2 = (f32[2,32,2,2,128,1,1]{4,1,2,0,3,6,5:T(8,128)S(1)}, f32[2,32,2,2,128,1,1]{4,1,2,0,3,6,5:T(8,128)}, u32[]{:S(2)}) copy-start(f32[2,32,2,2,128,1,1]{4,1,2,0,3,6,5:T(8,128)} %constant.301) | copy-start | bytes 393220
  383.6 98.2 %all-to-all-start.5 = ((bf16[32,2,2,128,128]{4,3,2,1,0:T(8,128)(2,1)}), bf16[32,2,2,128,128]{4,3,2,1,0:T(8,128)(2,1)}, u32[]{:S(2)}, u32[]{:S(2)}) async-start(bf16[32,2,2,128,128]{4,3,2,1,0:T(8,128)(2,1)} %copy.242), calls=%async_computation.5 | async-start | bytes 8388608 | tf_op jit(solution)/shard_map/all_to_all | solution.py:207
  418.9 16.5 %copy-start.6 = (f32[2,64,64,1,1]{1,2,0,4,3:T(8,128)S(1)}, f32[2,64,64,1,1]{1,2,0,4,3:T(8,128)}, u32[]{:S(2)}) copy-start(f32[2,64,64,1,1]{1,2,0,4,3:T(8,128)} %constant.302) | copy-start | bytes 98308
  481.8 64.1 %all-to-all-start.7 = ((s32[32,1,1]{2,1,0:T(1,128)}), s32[32,1,1]{2,1,0:T(1,128)S(1)}, u32[]{:S(2)}, u32[]{:S(2)}) async-start(s32[32,1,1]{2,1,0:T(1,128)} %copy.209), calls=%async_computation.7 | async-start | bytes 32768 | tf_op jit(solution)/shard_map/all_to_all | solution.py:264
  599.4 53.7 %all-to-all-start.6 = ((bf16[8,16,128,128]{3,2,1,0:T(8,128)(2,1)}), bf16[8,16,128,128]{3,2,1,0:T(8,128)(2,1)}, u32[]{:S(2)}, u32[]{:S(2)}) async-start(bf16[8,16,128,128]{3,2,1,0:T(8,128)(2,1)} %bitcast.333), calls=%async_computation.6 | async-start | bytes 8388608 | tf_op jit(solution)/shard_map/all_to_all | solution.py:228
  656.3 5.7 copy-start.8
  656.3 10.9 %copy-start.11 = (f32[2,2048]{1,0:T(2,128)S(1)}, f32[2,2048]{1,0:T(2,128)}, u32[]{:S(2)}) copy-start(f32[2,2048]{1,0:T(2,128)} %param.28) | copy-start | bytes 49156
  657.9 52.9 %all-to-all-start.9 = ((bf16[32,2,128,128]{3,2,1,0:T(8,128)(2,1)}), bf16[32,2,128,128]{3,2,1,0:T(8,128)(2,1)}, u32[]{:S(2)}, u32[]{:S(2)}) async-start(bf16[32,2,128,128]{3,2,1,0:T(8,128)(2,1)} %pad_maximum_fusion.4), calls=%async_computation.9 | async-start | bytes 4194304 | tf_op jit(solution)/shard_map/all_to_all | solution.py:267
  662.0 12.5 %copy-start.12 = (s32[2,2048]{1,0:T(2,128)S(1)}, s32[2,2048]{1,0:T(2,128)}, u32[]{:S(2)}) copy-start(s32[2,2048]{1,0:T(2,128)} %param.27) | copy-start | bytes 49156

commit v3 on v2

--- a/solution.py
+++ b/solution.py
@@ -155,6 +155,24 @@
     second = turned(second, twist, (high, 1, low))
     full = dot("cbdm,cknb->dknm", mixing(low, low, low, -1.0), second)
 
+    tile_rows = block_rows // TILE
+    tile_cols = block_cols // TILE
+    tile_groups = rows // TILE if rows % TILE == 0 else 1
+    wanted = tile_list[0]
+    tile_count = wanted.shape[0]
+    per_row = length // TILE
+    grid_row = wanted // per_row
+    grid_col = wanted % per_row
+    owner_index = grid_row // tile_rows * group_cols + grid_col // tile_cols
+    local_row = grid_row % tile_rows
+    local_index = (
+        local_row // tile_groups * tile_cols + grid_col % tile_cols
+    ) * tile_groups + local_row % tile_groups
+    owns = (owner_index[:, None] == jnp.arange(devices, dtype=jnp.int32)[None, :]).astype(jnp.int32)
+    request = jnp.sum(owns * (local_index[:, None] + 1), axis=0) - 1
+    request = lax.all_to_all(request, both, split_axis=0, concat_axis=0, tiled=True)
+    full, request = lax.optimization_barrier((full, request))
+
     row_index = (
         jnp.arange(high, dtype=jnp.int32)[:, None, None]
         + high * jnp.arange(low, dtype=jnp.int32)[None, None, :]
@@ -192,8 +210,6 @@
     real, imag = root(high, high, high, 1.0)
     end_table = np.stack([real, -imag]).astype(np.float32) / (length * length)
     first_k = (jnp.arange(high) == 0)[None, :, None, None]
-    tile_rows = block_rows // TILE
-    tile_cols = block_cols // TILE
 
     def columns_back(field):
         third = dot("cmdb,cknm->dknb", mixing(low, low, low, 1.0), field)
@@ -206,7 +222,7 @@
             back = back.reshape(devices, 1, 2, cols, rows)
         return lax.all_to_all(back, both, split_axis=0, concat_axis=0)
 
-    def rows_back(back, later):
+    def rows_back(back, later, before=None):
         groups, lanes = back.shape[1], back.shape[-1]
         if cols % high == 0:
             back = back.reshape(devices, groups, 2, cols // high, high, lanes)
@@ -225,29 +241,20 @@
         coeffs = coeffs.reshape(group_cols, tile_cols * groups, TILE, lanes)
         if later is not None:
             coeffs, later = lax.optimization_barrier((coeffs, later))
+        if before is not None:
+            coeffs, before = lax.optimization_barrier((coeffs, before))
         tiles = lax.all_to_all(coeffs, "gy", split_axis=0, concat_axis=0)
         if lanes != TILE:
             parts = TILE // lanes
             tiles = tiles.reshape(group_cols // parts, parts, tile_cols, TILE, lanes)
             tiles = tiles.transpose(0, 2, 3, 1, 4)
-        return tiles.reshape(tile_rows * tile_cols, TILE, TILE), later
+        return tiles.reshape(tile_rows * tile_cols, TILE, TILE), later, before
 
     received = [columns_back(field) for field in fields]
-    u_tiles, waiting = rows_back(received[0], received[1])
-    v_tiles, _ = rows_back(waiting, None)
+    u_tiles, waiting, _ = rows_back(received[0], received[1])
+    v_tiles, _, u_tiles = rows_back(waiting, None, u_tiles)
     tiles = [u_tiles, v_tiles]
-    tile_groups = rows // TILE if rows % TILE == 0 else 1
-
-    wanted = tile_list[0]
-    tile_count = wanted.shape[0]
-    per_row = length // TILE
-    grid_row = wanted // per_row
-    grid_col = wanted % per_row
-    owner_index = grid_row // tile_rows * group_cols + grid_col // tile_cols
-    local_row = grid_row % tile_rows
-    local_index = (
-        local_row // tile_groups * tile_cols + grid_col % tile_cols
-    ) * tile_groups + local_row % tile_groups
+
     float_total = float_slot.shape[0]
     capacity = 2 * float_total // tile_count
     member = (float_slot[:, None] == jnp.arange(tile_count, dtype=jnp.int32)[None, :]).astype(
@@ -259,9 +266,6 @@
     grouped_cell = grouped_cell.reshape(2, tile_count, capacity).transpose(1, 0, 2)
     grouped_frac = jnp.zeros((2, tile_count * capacity), F32).at[:, placing].set(float_frac)
     grouped_frac = grouped_frac.reshape(2, tile_count, capacity).transpose(1, 0, 2)
-    owns = (owner_index[:, None] == jnp.arange(devices, dtype=jnp.int32)[None, :]).astype(jnp.int32)
-    request = jnp.sum(owns * (local_index[:, None] + 1), axis=0) - 1
-    request = lax.all_to_all(request, both, split_axis=0, concat_axis=0, tiled=True)
     asked = jnp.maximum(request, 0)
     outgoing = jnp.stack([jnp.take(part, asked, axis=0) for part in tiles], axis=1)
     incoming = lax.all_to_all(outgoing, both, split_axis=0, concat_axis=0, tiled=True)

time: 742 us -> 694 us (0.935)
  blocking collectives: 53.5 us -> 0 us
    all_to_all x1 -> x0, blocking collectives: 53.5 us -> none  [rows_back(): tiles = lax.all_to_all(coeffs, 'gy', split_axis=0, concat_axis=0)]
    all_to_all x1 -> x2, waiting for transfers between devices: 45.5 us -> 46.1 us  [rows_back(): tiles = lax.all_to_all(coeffs, 'gy', split_axis=0, concat_axis=0)]
  transfers between devices with their start and end apart: 9 -> 10, of which waited for: 7 -> 7; matrix products, arithmetic and copies ran while one was open for 29% -> 36% of each run, Pallas kernels for 0% -> 0%
where the time goes in v3:
time: 694 us; the launch traced here: 683 us
  waiting for transfers between devices  281 us (40%)
  matrix products  131 us (19%)
  local copies, waits for them, and re-layouts  128 us (18%)
  other arithmetic  94.6 us (14%)
  starting transfers between devices  47.5 us (7%)
    dot_general x15, matrix products, dot(): jnp.einsum(formula, left, right, precision=HIGH, preferred_element_type=F32)  121 us
    all_to_all x2, waiting for transfers between devices, columns_back(): return lax.all_to_all(back, both, split_axis=0, concat_axis=0)  104 us
    all_to_all x2, waiting for transfers between devices, shards(): sent = lax.all_to_all(sent, both, split_axis=1, concat_axis=0)  83.3 us
    all_to_all x2, waiting for transfers between devices, rows_back(): tiles = lax.all_to_all(coeffs, 'gy', split_axis=0, concat_axis=0)  46.1 us
    another operation x7, other arithmetic, turned(): jnp.stack([values[0] * real - values[1] * imag, values[0] * imag + values...  35.5 us
    another operation x2, local copies, waits for them, and re-layouts, turned(): jnp.stack([values[0] * real - values[1] * imag, values[0] * imag + values...  33.2 us
    sub x6, other arithmetic, turned(): values[0] * real - values[1] * imag  26.7 us
    all_to_all x2, waiting for transfers between devices, shards(): lax.all_to_all(blocks[:, chunk].astype(F16), 'gy', split_axis=0, concat_a...  24.9 us
  transfers between devices with their start and end apart: 10, of which 7 were waited for; matrix products, arithmetic and copies ran while one was open for 36% of the time, Pallas kernels for 0%

profile of v3, /device:TPU:0, one launch (start us, length us, event | category | flops | bytes accessed | tf_op | source)
XLA Modules:
  0.0 682.9 jit_solution(13926933509728702677)
XLA Ops:
  14.6 24.9 %all-to-all-done = f16[8,128,1024]{2,1,0:T(8,128)(2,1)S(1)} async-done(((f16[8,128,1024]{2,1,0:T(8,128)(2,1)}), f16[8,128,1024]{2,1,0:T(8,128)(2,1)S(1)}, u32[]{:S(2)}, u32[]{:S(2)}) %all-to-all-start) | async-done | bytes 2097184 | tf_op jit(solution)/shard_map/all_to_all | solution.py:124
  58.2 8.8 %fusion.45 = f32[2,64,64,128]{3,1,2,0:T(8,128)S(1)} fusion(f32[2,128,2,64,1]{1,3,0,4,2:T(8,128)S(1)} %copy-done.4, f32[2,64,128,128]{3,1,2,0:T(8,128)S(1)} %pad_maximum_fusion.2), kind=kOutput, calls=%fused_computation.87 | convolution fusion | flops 1610612736 | bytes 12713984 | tf_op jit(solution)/shard_map/cbdm,ckrb->dmkr/dot_general | solution.py:38
  93.9 8.6 %fusion.48 = f32[2,64,64,128]{3,1,2,0:T(8,128)S(1)} fusion(f32[2,128,2,64,1]{1,3,0,4,2:T(8,128)S(1)} %copy-done.4, f32[2,64,128,128]{3,1,2,0:T(8,128)S(1)} %pad_maximum_fusion.3), kind=kOutput, calls=%fused_computation.88 | convolution fusion | flops 1610612736 | bytes 12713984 | tf_op jit(solution)/shard_map/cbdm,ckrb->dmkr/dot_general | solution.py:38
  122.7 42.7 %all-to-all-done.3 = f16[1,2,32,128,128]{4,1,3,0,2:T(2,128)(2,1)S(1)} async-done(((f16[1,2,32,128,128]{4,1,3,0,2:T(2,128)(2,1)}), f16[1,2,32,128,128]{4,1,3,0,2:T(2,128)(2,1)S(1)}, u32[]{:S(2)}, u32[]{:S(2)}) %all-to-all-start.3) | async-done | bytes 2097184 | tf_op jit(solution)/shard_map/all_to_all | solution.py:141
  177.7 40.6 %all-to-all-done.2 = f16[1,2,32,128,128]{4,1,3,0,2:T(2,128)(2,1)} async-done(((f16[1,2,32,128,128]{4,1,3,0,2:T(2,128)(2,1)}), f16[1,2,32,128,128]{4,1,3,0,2:T(2,128)(2,1)}, u32[]{:S(2)}, u32[]{:S(2)}) %all-to-all-start.2) | async-done | bytes 2097184 | tf_op jit(solution)/shard_map/all_to_all | solution.py:141
  218.3 10.0 %fusion.12 = f32[2,64,128,128]{3,1,2,0:T(8,128)S(1)} fusion(f32[128,128,2,64,1]{1,3,4,0,2:T(8,128)} %fusion.23, f32[2,32,2,64,1]{3,1,0,4,2:T(8,128)S(1)} %copy-done.9, f16[1,2,32,128,128]{4,1,3,0,2:T(2,128)(2,1)} %all-to-all-done.2), kind=kOutput, calls=%fused_computation.34 | convolution fusion | flops 809500672 | bytes 18907136 | tf_op jit(solution)/shard_map/csdk,scnb->dknb/dot_general | solution.py:38
  232.1 10.8 %fusion.34 = f32[2,64,128,128]{3,2,0,1:T(8,128)S(1)} fusion(f32[2,128,2,128,1]{3,1,0,2,4:T(8,128)S(1)} %copy-done.5, f32[2,64,128,128,1]{3,1,2,0,4:T(8,128)S(1)} %maximum_bitcast_fusion), kind=kOutput, calls=%fused_computation.82 | convolution fusion | flops 3221225472 | bytes 17039360 | tf_op jit(solution)/shard_map/cbdm,cknb->dknm/dot_general | solution.py:38
  273.1 11.7 %bitcast_convert_fusion.3 = bf16[128,128,2,64]{1,3,2,0:T(8,128)(2,1)S(1)} fusion(f32[2,64,2,64,1]{1,3,0,2,4:T(8,128)S(1)} %copy-done.3, f32[2,64,128,128,1]{3,2,0,1,4:T(8,128)S(1)} %maximum_bitcast_fusion.3), kind=kOutput, calls=%fused_computation.28 | convolution fusion | flops 1612709888 | bytes 12648448 | tf_op jit(solution)/shard_map/ckda,cknb->adnb/dot_general | solution.py:38
  300.1 11.7 %bitcast_convert_fusion.1 = bf16[128,128,2,64]{1,3,2,0:T(8,128)(2,1)S(1)} fusion(f32[2,64,2,64,1]{1,3,0,2,4:T(8,128)S(1)} %copy-done.3, f32[2,64,128,128,1]{3,2,0,1,4:T(8,128)S(1)} %maximum_bitcast_fusion.6), kind=kOutput, calls=%fused_computation.24 | convolution fusion | flops 1612709888 | bytes 12648448 | tf_op jit(solution)/shard_map/ckda,cknb->adnb/dot_general | solution.py:38
  318.7 71.0 %all-to-all-done.5 = bf16[32,2,2,128,128]{4,3,2,1,0:T(8,128)(2,1)} async-done(((bf16[32,2,2,128,128]{4,3,2,1,0:T(8,128)(2,1)}), bf16[32,2,2,128,128]{4,3,2,1,0:T(8,128)(2,1)}, u32[]{:S(2)}, u32[]{:S(2)}) %all-to-all-start.5) | async-done | bytes 4194336 | tf_op jit(solution)/shard_map/all_to_all | solution.py:223
  395.0 10.2 %convolution_bitcast_fusion.1 = f32[2,2,64,128,128]{3,4,0,2,1:T(8,128)S(1)} fusion(f32[2,32,2,2,128,1,1]{4,1,2,0,3,6,5:T(8,128)S(1)} %copy-done.2, bf16[32,2,2,2,64,128,1]{5,4,3,2,1,0,6:T(8,128)(2,1)} %bitcast.80), kind=kOutput, calls=%fused_computation.46 | convolution fusion | flops 3221225472 | bytes 21102592 | tf_op jit(solution)/shard_map/csmdb,sgcmky->dgkby/dot_general | solution.py:38
  405.2 7.2 %multiply_subtract_fusion.1 = (f32[1,2,64,128,128]{3,4,0,2,1:T(8,128)}, f32[1,2,64,128,128]{3,4,0,2,1:T(8,128)}) fusion(f32[2,2,64,128,128]{3,4,0,2,1:T(8,128)S(1)} %convolution_bitcast_fusion.1, f32[64,128]{1,0:T(8,128)S(1)} %get-tuple-element.101, f32[64,128]{1,0:T(8,128)S(1)} %get-tuple-element.102, f32[2,128,128]{1,2,0:T(8,128)S(1)} %broadcast_multiply_fusion.1, ...), kind=kLoop, calls=%fused_computation.44 | loop fusion | flops 16777216 | bytes 33751104 | tf_op jit(solution)/shard_map/sub | solution.py:44
  412.4 11.7 %pad_maximum_fusion = f32[2,2,64,128,128]{3,4,0,2,1:T(8,128)} fusion(f32[1,2,64,128,128]{3,4,0,2,1:T(8,128)} %get-tuple-element.35, f32[1,2,64,128,128]{3,4,0,2,1:T(8,128)} %get-tuple-element.34), kind=kLoop, calls=%fused_computation.6 | loop fusion | flops 4194304 | bytes 33554432 | tf_op jit(solution)/shard_map/stack | solution.py:43
  424.1 16.6 %copy.237 = f32[2,2,64,128,128]{4,2,0,3,1:T(8,128)} copy(f32[2,2,64,128,128]{3,4,0,2,1:T(8,128)} %pad_maximum_fusion) | data formatting | bytes 33554432 | tf_op jit(solution)/shard_map/stack | solution.py:43
  440.8 9.1 %fusion.19 = bf16[64,2,128,128]{3,0,2,1:T(8,128)(2,1)S(1)} fusion(f32[2,2,64,128,128]{4,2,0,3,1:T(8,128)} %copy.237, f32[2,64,64,1,1]{1,2,0,4,3:T(8,128)S(1)} %copy-done.6), kind=kOutput, calls=%fused_computation.47 | convolution fusion | flops 1612709888 | bytes 21004288 | tf_op jit(solution)/shard_map/cka,cgkby->agby/dot_general | solution.py:38
  454.5 33.4 %all-to-all-done.6 = bf16[32,2,2,128,128]{4,3,2,1,0:T(8,128)(2,1)} async-done(((bf16[32,2,2,128,128]{4,3,2,1,0:T(8,128)(2,1)}), bf16[32,2,2,128,128]{4,3,2,1,0:T(8,128)(2,1)}, u32[]{:S(2)}, u32[]{:S(2)}) %all-to-all-start.6) | async-done | bytes 4194336 | tf_op jit(solution)/shard_map/all_to_all | solution.py:223
  493.2 10.2 %convolution_bitcast_fusion = f32[2,2,64,128,128]{3,4,0,2,1:T(8,128)S(1)} fusion(f32[2,32,2,2,128,1,1]{4,1,2,0,3,6,5:T(8,128)S(1)} %copy-done.2, bf16[32,2,2,2,64,128,1]{5,4,3,2,1,0,6:T(8,128)(2,1)} %bitcast.109), kind=kOutput, calls=%fused_computation.45 | convolution fusion | flops 3221225472 | bytes 21102592 | tf_op jit(solution)/shard_map/csmdb,sgcmky->dgkby/dot_general | solution.py:38
  503.5 7.2 %multiply_subtract_fusion = (f32[1,2,64,128,128]{3,4,0,2,1:T(8,128)}, f32[1,2,64,128,128]{3,4,0,2,1:T(8,128)}) fusion(f32[2,2,64,128,128]{3,4,0,2,1:T(8,128)S(1)} %convolution_bitcast_fusion, f32[2,128,128]{1,2,0:T(8,128)S(1)} %broadcast_multiply_fusion, f32[64,128]{1,0:T(8,128)S(1)} %get-tuple-element.101, f32[64,128]{1,0:T(8,128)S(1)} %get-tuple-element.102, ...), kind=kLoop, calls=%fused_computation.42 | loop fusion | flops 16777216 | bytes 33751104 | tf_op jit(solution)/shard_map/sub | solution.py:44
  510.7 11.7 %pad_maximum_fusion.1 = f32[2,2,64,128,128]{3,4,0,2,1:T(8,128)} fusion(f32[1,2,64,128,128]{3,4,0,2,1:T(8,128)} %get-tuple-element.33, f32[1,2,64,128,128]{3,4,0,2,1:T(8,128)} %get-tuple-element.32), kind=kLoop, calls=%fused_computation.7 | loop fusion | flops 4194304 | bytes 33554432 | tf_op jit(solution)/shard_map/stack | solution.py:43
  522.4 16.6 %copy.244 = f32[2,2,64,128,128]{4,2,0,3,1:T(8,128)} copy(f32[2,2,64,128,128]{3,4,0,2,1:T(8,128)} %pad_maximum_fusion.1) | data formatting | bytes 33554432 | tf_op jit(solution)/shard_map/stack | solution.py:43
  539.0 8.9 %fusion.20 = bf16[64,2,128,128]{3,0,2,1:T(8,128)(2,1)S(1)} fusion(f32[2,2,64,128,128]{4,2,0,3,1:T(8,128)} %copy.244, f32[2,64,64,1,1]{1,2,0,4,3:T(8,128)S(1)} %copy-done.6), kind=kOutput, calls=%fused_computation.48 | convolution fusion | flops 1612709888 | bytes 21004288 | tf_op jit(solution)/shard_map/cka,cgkby->agby/dot_general | solution.py:38
  560.2 46.1 %all-to-all-done.8 = bf16[8,16,128,128]{3,2,1,0:T(8,128)(2,1)} async-done(((bf16[8,16,128,128]{3,2,1,0:T(8,128)(2,1)}), bf16[8,16,128,128]{3,2,1,0:T(8,128)(2,1)}, u32[]{:S(2)}, u32[]{:S(2)}) %all-to-all-start.8) | async-done | bytes 4194336 | tf_op jit(solution)/shard_map/all_to_all | solution.py:246
  640.9 22.5 %all-to-all-done.9 = bf16[32,2,128,128]{3,2,1,0:T(8,128)(2,1)} async-done(((bf16[32,2,128,128]{3,2,1,0:T(8,128)(2,1)}), bf16[32,2,128,128]{3,2,1,0:T(8,128)(2,1)}, u32[]{:S(2)}, u32[]{:S(2)}) %all-to-all-start.9) | async-done | bytes 2097184 | tf_op jit(solution)/shard_map/all_to_all | solution.py:271
  665.7 9.5 %fusion.27 = f32[16,2,256]{2,1,0:T(2,128)S(1)} fusion(f32[16,256,128]{1,2,0:T(8,128)} %copy.250, f32[16,256]{1,0:T(8,128)S(1)} %get-tuple-element.83, s32[16,256]{1,0:T(8,128)S(1)} %get-tuple-element.77, f32[16,256]{1,0:T(8,128)S(1)} %get-tuple-element.82, s32[16,256]{1,0:T(8,128)S(1)} %get-tuple-element.76, f32[16,256]{1,0:T(8,128)S(1)} %get-tuple-element.84, ...), kind=kOutput, calls=%fused_computation.58 | convolution fusion | flops 277340160 | bytes 3309584 | tf_op jit(solution)/shard_map/scr,sdtr->sdct/dot_general | solution.py:95
  (172 shorter events, 220.0 us)
Async XLA Ops:
  7.6 5.3 copy-start.14
  7.6 31.9 %all-to-all-start = ((f16[8,128,1024]{2,1,0:T(8,128)(2,1)}), f16[8,128,1024]{2,1,0:T(8,128)(2,1)S(1)}, u32[]{:S(2)}, u32[]{:S(2)}) async-start(f16[8,128,1024]{2,1,0:T(8,128)(2,1)} %get-tuple-element.57), calls=%async_computation | async-start | bytes 4194304 | tf_op jit(solution)/shard_map/all_to_all | solution.py:124
  39.5 32.7 %all-to-all-start.1 = ((f16[8,128,1024]{2,1,0:T(8,128)(2,1)}), f16[8,128,1024]{2,1,0:T(8,128)(2,1)}, u32[]{:S(2)}, u32[]{:S(2)}) async-start(f16[8,128,1024]{2,1,0:T(8,128)(2,1)} %get-tuple-element.56), calls=%async_computation.1 | async-start | bytes 4194304 | tf_op jit(solution)/shard_map/all_to_all | solution.py:124
  43.9 6.6 copy-start.7
  50.5 3.9 copy-start.13
  72.3 38.6 %all-to-all-start.4 = ((s32[32,1,1]{2,1,0:T(1,128)}), s32[32,1,1]{2,1,0:T(1,128)S(1)}, u32[]{:S(2)}, u32[]{:S(2)}) async-start(s32[32,1,1]{2,1,0:T(1,128)} %copy.227), calls=%async_computation.4 | async-start | bytes 32768 | tf_op jit(solution)/shard_map/all_to_all | solution.py:173
  110.8 54.6 %all-to-all-start.3 = ((f16[1,2,32,128,128]{4,1,3,0,2:T(2,128)(2,1)}), f16[1,2,32,128,128]{4,1,3,0,2:T(2,128)(2,1)S(1)}, u32[]{:S(2)}, u32[]{:S(2)}) async-start(f16[1,2,32,128,128]{4,1,3,0,2:T(2,128)(2,1)} %copy.222), calls=%async_computation.3 | async-start | bytes 4194304 | tf_op jit(solution)/shard_map/all_to_all | solution.py:141
  116.7 54.7 %copy-start.10 = (f32[2,32,2,64,1]{3,1,0,4,2:T(8,128)S(1)}, f32[2,32,2,64,1]{3,1,0,4,2:T(8,128)}, u32[]{:S(2)}) copy-start(f32[2,32,2,64,1]{3,1,0,4,2:T(8,128)} %constant.301) | copy-start | bytes 98308
  165.4 52.9 %all-to-all-start.2 = ((f16[1,2,32,128,128]{4,1,3,0,2:T(2,128)(2,1)}), f16[1,2,32,128,128]{4,1,3,0,2:T(2,128)(2,1)}, u32[]{:S(2)}, u32[]{:S(2)}) async-start(f16[1,2,32,128,128]{4,1,3,0,2:T(2,128)(2,1)} %copy.214), calls=%async_computation.2 | async-start | bytes 4194304 | tf_op jit(solution)/shard_map/all_to_all | solution.py:141
  171.4 47.0 %copy-start.9 = (f32[2,32,2,64,1]{3,1,0,4,2:T(8,128)S(1)}, f32[2,32,2,64,1]{3,1,0,4,2:T(8,128)}, u32[]{:S(2)}) copy-start(f32[2,32,2,64,1]{3,1,0,4,2:T(8,128)} %constant.300) | copy-start | bytes 98308
  251.1 5.5 copy-start.1
  291.6 98.1 %all-to-all-start.5 = ((bf16[32,2,2,128,128]{4,3,2,1,0:T(8,128)(2,1)}), bf16[32,2,2,128,128]{4,3,2,1,0:T(8,128)(2,1)}, u32[]{:S(2)}, u32[]{:S(2)}) async-start(bf16[32,2,2,128,128]{4,3,2,1,0:T(8,128)(2,1)} %copy.235), calls=%async_computation.5 | async-start | bytes 8388608 | tf_op jit(solution)/shard_map/all_to_all | solution.py:223
  318.7 76.3 %copy-start.2 = (f32[2,32,2,2,128,1,1]{4,1,2,0,3,6,5:T(8,128)S(1)}, f32[2,32,2,2,128,1,1]{4,1,2,0,3,6,5:T(8,128)}, u32[]{:S(2)}) copy-start(f32[2,32,2,2,128,1,1]{4,1,2,0,3,6,5:T(8,128)} %constant.305) | copy-start | bytes 393220
  389.7 98.2 %all-to-all-start.6 = ((bf16[32,2,2,128,128]{4,3,2,1,0:T(8,128)(2,1)}), bf16[32,2,2,128,128]{4,3,2,1,0:T(8,128)(2,1)}, u32[]{:S(2)}, u32[]{:S(2)}) async-start(bf16[32,2,2,128,128]{4,3,2,1,0:T(8,128)(2,1)} %copy.242), calls=%async_computation.6 | async-start | bytes 8388608 | tf_op jit(solution)/shard_map/all_to_all | solution.py:223
  424.1 16.6 %copy-start.6 = (f32[2,64,64,1,1]{1,2,0,4,3:T(8,128)S(1)}, f32[2,64,64,1,1]{1,2,0,4,3:T(8,128)}, u32[]{:S(2)}) copy-start(f32[2,64,64,1,1]{1,2,0,4,3:T(8,128)} %constant.306) | copy-start | bytes 98308
  487.9 64.7 %all-to-all-start.7 = ((bf16[8,16,128,128]{3,2,1,0:T(8,128)(2,1)}), bf16[8,16,128,128]{3,2,1,0:T(8,128)(2,1)}, u32[]{:S(2)}, u32[]{:S(2)}) async-start(bf16[8,16,128,128]{3,2,1,0:T(8,128)(2,1)} %bitcast.333), calls=%async_computation.7 | async-start | bytes 8388608 | tf_op jit(solution)/shard_map/all_to_all | solution.py:246
  552.5 4.7 copy-start.17
  552.5 53.8 %all-to-all-start.8 = ((bf16[8,16,128,128]{3,2,1,0:T(8,128)(2,1)}), bf16[8,16,128,128]{3,2,1,0:T(8,128)(2,1)}, u32[]{:S(2)}, u32[]{:S(2)}) async-start(bf16[8,16,128,128]{3,2,1,0:T(8,128)(2,1)} %bitcast.334), calls=%async_computation.8 | async-start | bytes 8388608 | tf_op jit(solution)/shard_map/all_to_all | solution.py:246
  609.5 5.0 copy-start.8
  609.6 10.2 %copy-start.11 = (f32[2,2048]{1,0:T(2,128)S(1)}, f32[2,2048]{1,0:T(2,128)}, u32[]{:S(2)}) copy-start(f32[2,2048]{1,0:T(2,128)} %param.28) | copy-start | bytes 49156
  611.1 52.3 %all-to-all-start.9 = ((bf16[32,2,128,128]{3,2,1,0:T(8,128)(2,1)}), bf16[32,2,128,128]{3,2,1,0:T(8,128)(2,1)}, u32[]{:S(2)}, u32[]{:S(2)}) async-start(bf16[32,2,128,128]{3,2,1,0:T(8,128)(2,1)} %pad_maximum_fusion.4), calls=%async_computation.9 | async-start | bytes 4194304 | tf_op jit(solution)/shard_map/all_to_all | solution.py:271
  614.6 12.5 %copy-start.12 = (s32[2,2048]{1,0:T(2,128)S(1)}, s32[2,2048]{1,0:T(2,128)}, u32[]{:S(2)}) copy-start(s32[2,2048]{1,0:T(2,128)} %param.27) | copy-start | bytes 49156
  633.6 7.2 %copy-start.15 = (s32[1,16]{1,0:T(1,128)S(1)}, s32[1,16]{1,0:T(1,128)}, u32[]{:S(2)}) copy-start(s32[1,16]{1,0:T(1,128)} %param.25) | copy-start | bytes 196
  634.3 31.5 %copy-start.16 = (pred[16]{0:T(512)(128)(4,1)S(1)}, pred[16]{0:T(512)(128)(4,1)}, u32[]{:S(2)}) copy-start(pred[16]{0:T(512)(128)(4,1)} %get-tuple-element.28) | copy-start | bytes 52
  (4 other events, 9.7 us)
